TPU v7x, 32 devices: a whole 2x2x4 slice. The times are simulated.
32 devices in a mesh: groups: 2 (over y), beam: 8 (over z, x), mp: 2 (over core).
Axes of the slice: x: 2, y: 2, z: 4, core: 2. Of those that a mesh axis runs over, the one named last changes fastest.
Arguments:
- states: float32 [64, 8, 128, 128], P(('groups', 'beam'), 'mp'), parts along dimension 0, may hold values from -4 to 4
- parent_beam: int32 [64], P(('groups', 'beam')), parts along dimension 0, may hold values from 0 to 7, as said below
- next_token: int32 [64], P(('groups', 'beam')), parts along dimension 0, may hold values from 0 to 1023
- proj_table: bfloat16 [1024, 8, 640], P('beam', 'mp'), may hold values from -6 to 6
- gate_table: bfloat16 [1024, 3, 8], P('beam', None, 'mp'), may hold values from -6 to 6
- gain: float32 [8, 128], P('mp'), may hold values from 0.1 to 1.9
Outputs:
- readout: bfloat16 [64, 8, 128], P(('groups', 'beam'), 'mp'), parts along dimension 0
- new_states: float32 [64, 8, 128, 128], P(('groups', 'beam'), 'mp'), parts along dimension 0
There are 2 independent parts, one for each index of `groups`. A program takes and returns all parts, laid end to end along the dimension named above; an argument that names none is the same for every part. Nothing has to cross between parts.
Inputs may be any that keep to these rules, and one draw needn't show every extreme that they name: The parent of hypothesis h = b * 4 + u is parent_beam[h] * 4 + u. In each aligned block of 4 hypotheses at most 2 take their parent from any one beam other than their own beam, and every block has a beam that supplies exactly 2.
All inputs are finite; a program needn't handle non-finite values.
Results may differ from a plain program's by a relative error of at most 0.001.
Values may be sent and summed in bfloat16 or wider, within the bound.
No kernel may reach another device: no remote copies, remote signals or barrier semaphores. Data moves between devices by JAX's collectives and lax.ppermute only.
A program may use at most 64 MiB of HBM per device.

v0:
```python
import jax
import jax.numpy as jnp
from jax import lax
from jax.sharding import PartitionSpec as P

HEAD_DIM = 128
BEAMS = 8
CAP = 2


def from_behind(block, axis, distance):
    devices = range(lax.axis_size(axis))
    route = [((i - distance) % len(devices), i) for i in devices]
    return lax.ppermute(block, axis, route)


def unit_norm(vector):
    return vector * lax.rsqrt(jnp.sum(vector * vector, axis=-1, keepdims=True) + 1e-06)


def advance(parents, entries, gate_entries, gain):
    retain = jax.nn.sigmoid(gate_entries[:, 0, :])
    strengths = 2.0 * jax.nn.sigmoid(gate_entries[:, 1:, :])
    state_now = retain[:, :, None, None] * parents
    for reflect in range(2):
        key_unit = unit_norm(entries[:, :, 1 + reflect, :])
        value_row = entries[:, :, 3 + reflect, :]
        applied = jnp.einsum("nhvd,nhd->nhv", state_now, key_unit, precision=lax.Precision.HIGHEST)
        state_now = (
            state_now
            - strengths[:, reflect, :, None, None]
            * (applied - value_row)[:, :, :, None]
            * key_unit[:, :, None, :]
        )
    query_unit = unit_norm(entries[:, :, 0, :])
    readout = jnp.einsum("nhvd,nhd->nhv", state_now, query_unit, precision=lax.Precision.HIGHEST)
    normed = (
        gain[None, :, :]
        * readout
        * lax.rsqrt(jnp.mean(readout * readout, axis=-1, keepdims=True) + 1e-05)
    )
    return (normed.astype(jnp.bfloat16), state_now)


def local(states, parent_beam, next_token, proj_table, gate_table, gain):
    hyp_rows = states.shape[0]
    head_count = states.shape[1]
    devices = lax.axis_size("beam")
    spacing = devices // BEAMS
    position = lax.axis_index("beam")
    my_beam = position // spacing
    offset = (my_beam - parent_beam) % BEAMS
    tokens_all, parents_all = (
        lax.all_gather(next_token, "beam", axis=0, tiled=True),
        lax.all_gather(parent_beam, "beam", axis=0, tiled=True),
    )
    vocab_rows = proj_table.shape[0]
    local_ids = tokens_all - position * vocab_rows
    onehot = (local_ids[:, None] == jnp.arange(vocab_rows, dtype=jnp.int32)[None, :]).astype(
        jnp.bfloat16
    )
    flat_table = proj_table.reshape(vocab_rows, head_count * 5 * HEAD_DIM)
    flat_gates = gate_table.reshape(vocab_rows, 3 * head_count)
    looked = jnp.dot(onehot, flat_table, preferred_element_type=jnp.float32).astype(jnp.bfloat16)
    looked_gates = jnp.dot(onehot, flat_gates, preferred_element_type=jnp.float32).astype(
        jnp.bfloat16
    )
    looked = looked.reshape(devices, hyp_rows, head_count * 5 * HEAD_DIM)
    looked_gates = looked_gates.reshape(devices, hyp_rows, 3 * head_count)
    arrived, arrived_gates = (
        lax.all_to_all(looked, "beam", split_axis=0, concat_axis=0, tiled=True),
        lax.all_to_all(looked_gates, "beam", split_axis=0, concat_axis=0, tiled=True),
    )
    entries = jnp.sum(arrived, axis=0, dtype=jnp.float32).reshape(hyp_rows, head_count, 5, HEAD_DIM)
    gate_entries = jnp.sum(arrived_gates, axis=0, dtype=jnp.float32).reshape(
        hyp_rows, 3, head_count
    )
    parents = jnp.where((offset == 0)[:, None, None, None], states, jnp.zeros_like(states))
    slot_ids = jnp.arange(CAP, dtype=jnp.int32)
    for distance in range(1, BEAMS):
        target = (position + distance * spacing) % devices
        their_parents = lax.dynamic_slice_in_dim(parents_all, target * hyp_rows, hyp_rows)
        needed = their_parents == my_beam
        slot_rank = jnp.cumsum(needed.astype(jnp.int32)) - 1
        select = ((slot_rank[None, :] == slot_ids[:, None]) & needed[None, :]).astype(jnp.float32)
        packed = jnp.einsum("cr,rhij->chij", select, states, precision=lax.Precision.HIGHEST)
        received = from_behind(packed, "beam", distance * spacing)
        wanted = offset == distance
        wanted_rank = jnp.cumsum(wanted.astype(jnp.int32)) - 1
        placing = ((wanted_rank[:, None] == slot_ids[None, :]) & wanted[:, None]).astype(
            jnp.float32
        )
        parents = parents + jnp.einsum(
            "rc,chij->rhij", placing, received, precision=lax.Precision.HIGHEST
        )
    return advance(parents, entries, gate_entries, gain)


def solution(mesh):
    return jax.shard_map(
        local,
        mesh=mesh,
        in_specs=(
            P(("groups", "beam"), "mp", None, None),
            P(("groups", "beam")),
            P(("groups", "beam")),
            P("beam", "mp", None),
            P("beam", None, "mp"),
            P("mp", None),
        ),
        out_specs=(P(("groups", "beam"), "mp", None), P(("groups", "beam"), "mp", None, None)),
        check_vma=False,
    )
```

profile of v0, /device:TPU:0, one launch (start us, length us, event | category | flops | bytes accessed | tf_op | source)
XLA Modules:
  0.0 151.5 jit_solution(17628549391322259586)
XLA Ops:
  2.5 0.9 dynamic-update-slice
  3.4 0.8 dynamic-update-slice.1
  4.2 13.1 %all-reduce.2 = (s32[32]{0:T(128)S(1)}, s32[32]{0:T(128)S(1)}) all-reduce(s32[32]{0:T(128)S(1)} %dynamic-update-slice.1, s32[32]{0:T(128)S(1)} %dynamic-update-slice), channel_id=1, replica_groups=mesh['groups'=2,'beam'=8,'mp'=2] {'beam'}, use_global_device_ids=true, to_apply=%add.1 | all-reduce | flops 64 | bytes 512
  17.6 3.7 %fusion.13 = f32[2,4,128,128]{3,0,2,1:T(2,128)} fusion(f32[4,4,128,128]{3,2,1,0:T(8,128)} %param.6, pred[4]{0:T(512)(128)(4,1)S(1)} %get-tuple-element.56, s32[4]{0:T(128)S(1)} %add_bitcast_fusion.2), kind=kOutput, calls=%fused_computation.19 | convolution fusion | flops 6291472 | bytes 1572884 | tf_op jit(solution)/shard_map/cr,rhij->chij/dot_general | solution.py:86
  21.5 2.5 %fusion.15 = f32[2,4,128,128]{3,0,2,1:T(2,128)} fusion(f32[4,4,128,128]{3,2,1,0:T(8,128)S(1)} %copy-done, pred[4]{0:T(512)(128)(4,1)S(1)} %get-tuple-element.54, s32[4]{0:T(128)S(1)} %add_bitcast_fusion.4), kind=kOutput, calls=%fused_computation.21 | convolution fusion | flops 6291472 | bytes 1572884 | tf_op jit(solution)/shard_map/cr,rhij->chij/dot_general | solution.py:86
  23.9 2.8 %collective-permute-start.4 = (f32[2,4,128,128]{3,0,2,1:T(2,128)}, f32[2,4,128,128]{3,0,2,1:T(2,128)S(1)}, u32[]{:S(2)}, u32[]{:S(2)}) collective-permute-start(f32[2,4,128,128]{3,0,2,1:T(2,128)} %fusion.15), channel_id=1, source_target_pairs={{6,0},{8,2},{10,4},{12,6},{14,8},{0,10},{2,12},{4,14},{7,1},{9,3},... | collective-permute-start | bytes 1572872 | tf_op jit(solution)/shard_map/ppermute | solution.py:14
  27.0 1.7 %fusion.17 = f32[2,4,128,128]{3,0,2,1:T(2,128)S(1)} fusion(f32[4,4,128,128]{3,2,1,0:T(8,128)S(1)} %copy-done, pred[4]{0:T(512)(128)(4,1)S(1)} %get-tuple-element.52, s32[4]{0:T(128)S(1)} %add_bitcast_fusion.6), kind=kOutput, calls=%fused_computation.23 | convolution fusion | flops 6291472 | bytes 1572884 | tf_op jit(solution)/shard_map/cr,rhij->chij/dot_general | solution.py:86
  28.6 1.3 collective-permute-start.3
  30.1 2.5 %fusion.19 = f32[2,4,128,128]{3,0,2,1:T(2,128)} fusion(f32[4,4,128,128]{3,2,1,0:T(8,128)S(1)} %copy-done, pred[4]{0:T(512)(128)(4,1)S(1)} %get-tuple-element.50, s32[4]{0:T(128)S(1)} %add_bitcast_fusion.8), kind=kOutput, calls=%fused_computation.25 | convolution fusion | flops 6291472 | bytes 1572884 | tf_op jit(solution)/shard_map/cr,rhij->chij/dot_general | solution.py:86
  33.5 2.5 %fusion.21 = f32[2,4,128,128]{3,0,2,1:T(2,128)} fusion(f32[4,4,128,128]{3,2,1,0:T(8,128)S(1)} %copy-done, pred[4]{0:T(512)(128)(4,1)S(1)} %get-tuple-element.48, s32[4]{0:T(128)S(1)} %add_bitcast_fusion.10), kind=kOutput, calls=%fused_computation.27 | convolution fusion | flops 6291472 | bytes 1572884 | tf_op jit(solution)/shard_map/cr,rhij->chij/dot_general | solution.py:86
  36.0 1.4 collective-permute-start.1
  38.3 5.7 %all-to-all-start = ((bf16[8,4,12]{2,1,0:T(4,128)(2,1)}), bf16[8,4,12]{2,1,0:T(4,128)(2,1)S(1)}, u32[]{:S(2)}, u32[]{:S(2)}) async-start(bf16[8,4,12]{2,1,0:T(4,128)(2,1)} %bitcast.1), calls=%async_computation | async-start | bytes 16384 | tf_op jit(solution)/shard_map/all_to_all | solution.py:72
  45.8 1.7 %fusion.23 = f32[2,4,128,128]{3,0,2,1:T(2,128)S(1)} fusion(f32[4,4,128,128]{3,2,1,0:T(8,128)S(1)} %copy-done, pred[4]{0:T(512)(128)(4,1)S(1)} %get-tuple-element.11, s32[4]{0:T(128)S(1)} %add_bitcast_fusion.12), kind=kOutput, calls=%fused_computation.29 | convolution fusion | flops 6291472 | bytes 1572884 | tf_op jit(solution)/shard_map/cr,rhij->chij/dot_general | solution.py:86
  47.5 2.5 %fusion.11 = f32[2,4,128,128]{3,0,2,1:T(2,128)} fusion(f32[4,4,128,128]{3,2,1,0:T(8,128)S(1)} %copy-done, pred[4]{0:T(512)(128)(4,1)S(1)} %get-tuple-element.58, s32[4]{0:T(128)S(1)} %add_bitcast_fusion), kind=kOutput, calls=%fused_computation.17 | convolution fusion | flops 6291472 | bytes 1572884 | tf_op jit(solution)/shard_map/cr,rhij->chij/dot_general | solution.py:86
  50.8 50.1 %all-to-all-done = bf16[8,4,12]{2,1,0:T(4,128)(2,1)S(1)} async-done(((bf16[8,4,12]{2,1,0:T(4,128)(2,1)}), bf16[8,4,12]{2,1,0:T(4,128)(2,1)S(1)}, u32[]{:S(2)}, u32[]{:S(2)}) %all-to-all-start) | async-done | bytes 800 | tf_op jit(solution)/shard_map/all_to_all | solution.py:72
  101.0 3.4 %all-to-all-start.1 = ((bf16[8,4,2560]{2,1,0:T(4,128)(2,1)}), bf16[8,4,2560]{2,1,0:T(4,128)(2,1)S(1)}, u32[]{:S(2)}, u32[]{:S(2)}) async-start(bf16[8,4,2560]{2,1,0:T(4,128)(2,1)} %reshape.478), calls=%async_computation.1 | async-start | bytes 327680 | tf_op jit(solution)/shard_map/all_to_all | solution.py:71
  104.6 7.3 %all-to-all-done.1 = bf16[8,4,2560]{2,1,0:T(4,128)(2,1)S(1)} async-done(((bf16[8,4,2560]{2,1,0:T(4,128)(2,1)}), bf16[8,4,2560]{2,1,0:T(4,128)(2,1)S(1)}, u32[]{:S(2)}, u32[]{:S(2)}) %all-to-all-start.1) | async-done | bytes 163872 | tf_op jit(solution)/shard_map/all_to_all | solution.py:71
  112.7 0.9 collective-permute-start
  113.7 1.3 fusion.38
  115.0 4.1 %collective-permute-start.6 = (f32[2,4,128,128]{3,0,2,1:T(2,128)S(1)}, f32[2,4,128,128]{3,0,2,1:T(2,128)S(1)}, u32[]{:S(2)}, u32[]{:S(2)}) collective-permute-start(f32[2,4,128,128]{3,0,2,1:T(2,128)S(1)} %copy-done.3), channel_id=1, source_target_pairs={{2,0},{4,2},{6,4},{8,6},{10,8},{12,10},{14,12},{0,14},{3,1},{5,3},... | collective-permute-start | bytes 1572872 | tf_op jit(solution)/shard_map/ppermute | solution.py:14
  119.0 1.3 fusion.41
  120.3 2.3 %fusion.44 = f32[4,4,128,128]{3,0,2,1:T(4,128)S(1)} fusion(f32[2,4,128,128]{3,0,2,1:T(2,128)} %collective-permute-done.3, pred[4]{0:T(512)(128)(4,1)S(1)} %get-tuple-element.43, s32[4]{0:T(128)S(1)} %add_bitcast_fusion.7), kind=kOutput, calls=%fused_computation.72 | convolution fusion | flops 6291472 | bytes 1572884 | tf_op jit(solution)/shard_map/rc,chij->rhij/dot_general | solution.py:93
  122.7 2.3 %fusion.47 = f32[4,4,128,128]{3,0,2,1:T(4,128)S(1)} fusion(f32[2,4,128,128]{3,0,2,1:T(2,128)} %collective-permute-done.2, pred[4]{0:T(512)(128)(4,1)S(1)} %get-tuple-element.44, s32[4]{0:T(128)S(1)} %add_bitcast_fusion.9), kind=kOutput, calls=%fused_computation.75 | convolution fusion | flops 6291472 | bytes 1572884 | tf_op jit(solution)/shard_map/rc,chij->rhij/dot_general | solution.py:93
  125.1 2.3 %fusion.50 = f32[4,4,128,128]{3,0,2,1:T(4,128)S(1)} fusion(f32[2,4,128,128]{3,0,2,1:T(2,128)} %collective-permute-done.1, pred[4]{0:T(512)(128)(4,1)S(1)} %get-tuple-element.45, s32[4]{0:T(128)S(1)} %add_bitcast_fusion.11), kind=kOutput, calls=%fused_computation.78 | convolution fusion | flops 6291472 | bytes 1572884 | tf_op jit(solution)/shard_map/rc,chij->rhij/dot_general | solution.py:93
  127.4 10.4 %collective-permute-done.6 = f32[2,4,128,128]{3,0,2,1:T(2,128)S(1)} collective-permute-done((f32[2,4,128,128]{3,0,2,1:T(2,128)S(1)}, f32[2,4,128,128]{3,0,2,1:T(2,128)S(1)}, u32[]{:S(2)}, u32[]{:S(2)}) %collective-permute-start.6) | collective-permute-done | bytes 524320 | tf_op jit(solution)/shard_map/ppermute | solution.py:14
  137.8 1.3 fusion.35
  139.2 2.7 %fusion.6 = f32[4,4,128,128]{3,0,2,1:T(4,128)S(1)} fusion(f32[4,4,128,128]{3,0,2,1:T(4,128)S(1)} %fusion.35, f32[4,4,128,128]{3,0,2,1:T(4,128)S(1)} %fusion.38, f32[4,4,128,128]{3,0,2,1:T(4,128)S(1)} %fusion.41, f32[4,4,128,128]{3,0,2,1:T(4,128)S(1)} %fusion.44, f32[4,4,128,128]{3,0,2,1:T(4,128)S(1)} %fusion.47, f32[4,4,128,128]{3,0,2,1:T(4,128)S(1)} %fusion.50, ...), kind=kOutput, calls=%fused_computation.8 | convolution fusion | flops 8650768 | bytes 8912984 | tf_op jit(solution)/shard_map/rc,chij->rhij/dot_general | solution.py:93
  141.9 1.7 %fusion.9 = f32[4,4,1,128]{3,2,1,0:T(1,128)S(1)} fusion(f32[4,4,128,1]{2,3,1,0:T(1,128)S(1)} %bitcast.181, f32[4,4,128,128]{3,0,2,1:T(4,128)S(1)} %fusion.6), kind=kOutput, calls=%fused_computation.12 | convolution fusion | flops 3145728 | bytes 1064960 | tf_op jit(solution)/shard_map/nhvd,nhd->nhv/dot_general | solution.py:28
  143.9 1.0 multiply_subtract_fusion.1
  144.9 1.7 %fusion.7 = f32[4,4,1,128]{3,2,1,0:T(1,128)S(1)} fusion(f32[4,4,128,1]{2,3,1,0:T(1,128)S(1)} %bitcast.182, f32[4,4,128,128]{3,0,2,1:T(4,128)S(1)} %multiply_subtract_fusion.1), kind=kOutput, calls=%fused_computation.10 | convolution fusion | flops 3145728 | bytes 1064960 | tf_op jit(solution)/shard_map/nhvd,nhd->nhv/dot_general | solution.py:28
  146.8 1.4 multiply_subtract_fusion
  148.3 1.7 %fusion.128 = f32[4,4,1,128]{3,2,1,0:T(1,128)S(1)} fusion(f32[4,4,128,128]{3,2,1,0:T(8,128)S(1)} %copy.22, f32[4,4,128,1]{2,3,1,0:T(1,128)S(1)} %bitcast.180), kind=kOutput, calls=%fused_computation.201 | convolution fusion | flops 3145728 | bytes 1064960 | tf_op jit(solution)/shard_map/nhvd,nhd->nhv/dot_general | solution.py:36
  (93 shorter events, 9.5 us)
Async XLA Ops:
  0.6 0.7 copy-start.7
  0.6 20.8 %copy-start = (f32[4,4,128,128]{3,2,1,0:T(8,128)S(1)}, f32[4,4,128,128]{3,2,1,0:T(8,128)}, u32[]{:S(2)}) copy-start(f32[4,4,128,128]{3,2,1,0:T(8,128)} %param.6) | copy-start | bytes 3145732
  21.3 91.4 %collective-permute-start.5 = (f32[2,4,128,128]{3,0,2,1:T(2,128)}, f32[2,4,128,128]{3,0,2,1:T(2,128)S(1)}, u32[]{:S(2)}, u32[]{:S(2)}) collective-permute-start(f32[2,4,128,128]{3,0,2,1:T(2,128)} %fusion.13), channel_id=1, source_target_pairs={{4,0},{6,2},{8,4},{10,6},{12,8},{14,10},{0,12},{2,14},{5,1},{7,3},... | collective-permute-start | bytes 1572872 | tf_op jit(solution)/shard_map/ppermute | solution.py:14
  23.9 91.0 %collective-permute-start.4 = (f32[2,4,128,128]{3,0,2,1:T(2,128)}, f32[2,4,128,128]{3,0,2,1:T(2,128)S(1)}, u32[]{:S(2)}, u32[]{:S(2)}) collective-permute-start(f32[2,4,128,128]{3,0,2,1:T(2,128)} %fusion.15), channel_id=1, source_target_pairs={{6,0},{8,2},{10,4},{12,6},{14,8},{0,10},{2,12},{4,14},{7,1},{9,3},... | collective-permute-start | bytes 1572872 | tf_op jit(solution)/shard_map/ppermute | solution.py:14
  28.6 91.7 %collective-permute-start.3 = (f32[2,4,128,128]{3,0,2,1:T(2,128)S(1)}, f32[2,4,128,128]{3,0,2,1:T(2,128)}, u32[]{:S(2)}, u32[]{:S(2)}) collective-permute-start(f32[2,4,128,128]{3,0,2,1:T(2,128)S(1)} %fusion.17), channel_id=1, source_target_pairs={{8,0},{10,2},{12,4},{14,6},{0,8},{2,10},{4,12},{6,14},{9,1},{11,3}... | collective-permute-start | bytes 1572872 | tf_op jit(solution)/shard_map/ppermute | solution.py:14
  32.6 90.1 %collective-permute-start.2 = (f32[2,4,128,128]{3,0,2,1:T(2,128)}, f32[2,4,128,128]{3,0,2,1:T(2,128)}, u32[]{:S(2)}, u32[]{:S(2)}) collective-permute-start(f32[2,4,128,128]{3,0,2,1:T(2,128)} %fusion.19), channel_id=1, source_target_pairs={{10,0},{12,2},{14,4},{0,6},{2,8},{4,10},{6,12},{8,14},{11,1},{13,3... | collective-permute-start | bytes 1572872 | tf_op jit(solution)/shard_map/ppermute | solution.py:14
  33.5 3.8 %copy-start.4 = (bf16[128,3,4]{0,2,1:T(4,128)(2,1)S(1)}, bf16[128,3,4]{0,2,1:T(4,128)(2,1)}, u32[]{:S(2)}) copy-start(bf16[128,3,4]{0,2,1:T(4,128)(2,1)} %param.10) | copy-start | bytes 9220
  33.5 12.0 %copy-start.2 = (bf16[128,4,640]{2,1,0:T(4,128)(2,1)S(1)}, bf16[128,4,640]{2,1,0:T(4,128)(2,1)}, u32[]{:S(2)}) copy-start(bf16[128,4,640]{2,1,0:T(4,128)(2,1)} %param.9) | copy-start | bytes 1966084
  36.0 89.1 %collective-permute-start.1 = (f32[2,4,128,128]{3,0,2,1:T(2,128)}, f32[2,4,128,128]{3,0,2,1:T(2,128)}, u32[]{:S(2)}, u32[]{:S(2)}) collective-permute-start(f32[2,4,128,128]{3,0,2,1:T(2,128)} %fusion.21), channel_id=1, source_target_pairs={{12,0},{14,2},{0,4},{2,6},{4,8},{6,10},{8,12},{10,14},{13,1},{15,3... | collective-permute-start | bytes 1572872 | tf_op jit(solution)/shard_map/ppermute | solution.py:14
  38.3 5.7 %copy-start.6 = (s32[4]{0:T(128)S(1)}, s32[4]{0:T(128)}, u32[]{:S(2)}) copy-start(s32[4]{0:T(128)} %param.7) | copy-start | bytes 52
  38.3 62.7 %all-to-all-start = ((bf16[8,4,12]{2,1,0:T(4,128)(2,1)}), bf16[8,4,12]{2,1,0:T(4,128)(2,1)S(1)}, u32[]{:S(2)}, u32[]{:S(2)}) async-start(bf16[8,4,12]{2,1,0:T(4,128)(2,1)} %bitcast.1), calls=%async_computation | async-start | bytes 16384 | tf_op jit(solution)/shard_map/all_to_all | solution.py:72
  101.0 11.0 %all-to-all-start.1 = ((bf16[8,4,2560]{2,1,0:T(4,128)(2,1)}), bf16[8,4,2560]{2,1,0:T(4,128)(2,1)S(1)}, u32[]{:S(2)}, u32[]{:S(2)}) async-start(bf16[8,4,2560]{2,1,0:T(4,128)(2,1)} %reshape.478), calls=%async_computation.1 | async-start | bytes 327680 | tf_op jit(solution)/shard_map/all_to_all | solution.py:71
  112.7 26.4 %collective-permute-start = (f32[2,4,128,128]{3,0,2,1:T(2,128)S(1)}, f32[2,4,128,128]{3,0,2,1:T(2,128)S(1)}, u32[]{:S(2)}, u32[]{:S(2)}) collective-permute-start(f32[2,4,128,128]{3,0,2,1:T(2,128)S(1)} %fusion.23), channel_id=1, source_target_pairs={{14,0},{0,2},{2,4},{4,6},{6,8},{8,10},{10,12},{12,14},{15,1},{1,3}... | collective-permute-start | bytes 1572872 | tf_op jit(solution)/shard_map/ppermute | solution.py:14
  113.7 1.3 copy-start.3
  115.0 22.9 %collective-permute-start.6 = (f32[2,4,128,128]{3,0,2,1:T(2,128)S(1)}, f32[2,4,128,128]{3,0,2,1:T(2,128)S(1)}, u32[]{:S(2)}, u32[]{:S(2)}) collective-permute-start(f32[2,4,128,128]{3,0,2,1:T(2,128)S(1)} %copy-done.3), channel_id=1, source_target_pairs={{2,0},{4,2},{6,4},{8,6},{10,8},{12,10},{14,12},{0,14},{3,1},{5,3},... | collective-permute-start | bytes 1572872 | tf_op jit(solution)/shard_map/ppermute | solution.py:14
  148.3 3.2 %copy-start.1 = (f32[4,4,128,128]{3,2,1,0:T(8,128)}, f32[4,4,128,128]{3,2,1,0:T(8,128)S(1)}, u32[]{:S(2)}) copy-start(f32[4,4,128,128]{3,2,1,0:T(8,128)S(1)} %copy.22) | copy-start | bytes 3145732
  150.1 0.7 copy-start.5
where the time goes:
time: 152 us
  waiting for transfers between devices  67.9 us (45%)
  matrix products  36.1 us (24%)
  starting transfers between devices  20.4 us (13%)
  blocking collectives  13.1 us (9%)
  other arithmetic  6.68 us (4%)
  local copies, waits for them, and re-layouts  5.66 us (4%)
  between operations  1.7 us (1%)
    all_to_all x1, waiting for transfers between devices, local(): lax.all_to_all(looked_gates, 'beam', split_axis=0, concat_axis=0, tiled=T...  50.1 us
    dot_general x7, matrix products, local(): jnp.einsum('cr,rhij->chij', select, states, precision=lax.Precision.HIGHEST)  16.9 us
    dot_general x7, matrix products, local(): jnp.einsum('rc,chij->rhij', placing, received, precision=lax.Precision.HI...  13.7 us
    unnamed x1, blocking collectives  13.1 us
    ppermute x7, starting transfers between devices, from_behind(): return lax.ppermute(block, axis, route)  11.3 us
    ppermute x7, waiting for transfers between devices, from_behind(): return lax.ppermute(block, axis, route)  10.4 us
    all_to_all x1, waiting for transfers between devices, local(): lax.all_to_all(looked, 'beam', split_axis=0, concat_axis=0, tiled=True)  7.32 us
    all_to_all x1, starting transfers between devices, local(): lax.all_to_all(looked_gates, 'beam', split_axis=0, concat_axis=0, tiled=T...  5.71 us
  transfers between devices with their start and end apart: 9, of which 3 were waited for; matrix products, arithmetic and copies ran while one was open for 19% of the time, Pallas kernels for 0%

commit v1 on v0

v1 whole, which is shorter than its diff:
```python
import jax
import jax.numpy as jnp
from jax import lax
from jax.sharding import PartitionSpec as P

HEAD_DIM = 128
BEAMS = 8
FAR, NEAR, SIDE = 4, 2, 1
WIRE = jnp.float16
CHUNKS = 2


def swap(block, mask):
    devices = lax.axis_size("beam")
    spacing = devices // BEAMS
    route = [(i, ((i // spacing) ^ mask) * spacing + i % spacing) for i in range(devices)]
    return lax.ppermute(block, "beam", route)


def unit_norm(vector):
    return vector * lax.rsqrt(jnp.sum(vector * vector, axis=-1, keepdims=True) + 1e-06)


def advance(parents, entries, gate_entries, gain):
    retain = jax.nn.sigmoid(gate_entries[:, 0, :])
    strengths = 2.0 * jax.nn.sigmoid(gate_entries[:, 1:, :])
    state_now = retain[:, :, None, None] * parents
    for reflect in range(2):
        key_unit = unit_norm(entries[:, :, 1 + reflect, :])
        value_row = entries[:, :, 3 + reflect, :]
        applied = jnp.einsum("nhvd,nhd->nhv", state_now, key_unit, precision=lax.Precision.HIGHEST)
        state_now = (
            state_now
            - strengths[:, reflect, :, None, None]
            * (applied - value_row)[:, :, :, None]
            * key_unit[:, :, None, :]
        )
    query_unit = unit_norm(entries[:, :, 0, :])
    readout = jnp.einsum("nhvd,nhd->nhv", state_now, query_unit, precision=lax.Precision.HIGHEST)
    normed = (
        gain[None, :, :]
        * readout
        * lax.rsqrt(jnp.mean(readout * readout, axis=-1, keepdims=True) + 1e-05)
    )
    return (normed.astype(jnp.bfloat16), state_now)


def look_up(next_token, proj_table, gate_table):
    hyp_rows = next_token.shape[0]
    devices = lax.axis_size("beam")
    vocab_rows, head_count = proj_table.shape[:2]
    tokens = lax.all_to_all(
        jnp.broadcast_to(next_token[None, :], (devices, hyp_rows)), "beam", 0, 0, tiled=True
    ).reshape(devices * hyp_rows)
    local_ids = tokens - lax.axis_index("beam") * vocab_rows
    onehot = (local_ids[:, None] == jnp.arange(vocab_rows, dtype=jnp.int32)[None, :]).astype(
        jnp.bfloat16
    )
    width = head_count * 5 * HEAD_DIM
    looked = jnp.dot(
        onehot, proj_table.reshape(vocab_rows, width), preferred_element_type=jnp.float32
    ).astype(jnp.bfloat16)
    looked_gates = jnp.dot(
        onehot, gate_table.reshape(vocab_rows, 3 * head_count), preferred_element_type=jnp.float32
    ).astype(jnp.bfloat16)
    rows = jnp.concatenate([looked, looked_gates], axis=1).reshape(devices, hyp_rows, -1)
    arrived = lax.all_to_all(rows, "beam", split_axis=0, concat_axis=0, tiled=True)
    summed = jnp.sum(arrived, axis=0, dtype=jnp.float32)
    entries = summed[:, :width].reshape(hyp_rows, head_count, 5, HEAD_DIM)
    gate_entries = summed[:, width:].reshape(hyp_rows, 3, head_count)
    return entries, gate_entries


def pick(near, far, far_side, side, relation):
    rel = relation[:, None, None, None]
    return jnp.where(
        (rel & FAR) != 0,
        jnp.where((rel & SIDE) != 0, far_side, far),
        jnp.where((rel & SIDE) != 0, side, near),
    )


def local(states, parent_beam, next_token, proj_table, gate_table, gain):
    devices = lax.axis_size("beam")
    my_beam = lax.axis_index("beam") // (devices // BEAMS)
    relation = parent_beam ^ my_beam
    peer_relation = swap(parent_beam, NEAR) ^ my_beam
    entries, gate_entries = look_up(next_token, proj_table, gate_table)
    head_count = states.shape[1]
    step = head_count // CHUNKS
    parents = []
    for chunk in range(CHUNKS):
        exact = states[:, chunk * step : (chunk + 1) * step]
        near = exact.astype(WIRE)
        far = swap(near, FAR)
        side = swap(near, SIDE)
        far_side = swap(far, SIDE)
        block = swap(pick(near, far, far_side, side, peer_relation), NEAR)
        mine = pick(
            exact,
            far.astype(jnp.float32),
            far_side.astype(jnp.float32),
            side.astype(jnp.float32),
            relation,
        )
        crossed = (relation & NEAR)[:, None, None, None] != 0
        parents.append(jnp.where(crossed, block.astype(jnp.float32), mine))
    return advance(jnp.concatenate(parents, axis=1), entries, gate_entries, gain)


def solution(mesh):
    return jax.shard_map(
        local,
        mesh=mesh,
        in_specs=(
            P(("groups", "beam"), "mp", None, None),
            P(("groups", "beam")),
            P(("groups", "beam")),
            P("beam", "mp", None),
            P("beam", None, "mp"),
            P("mp", None),
        ),
        out_specs=(P(("groups", "beam"), "mp", None), P(("groups", "beam"), "mp", None, None)),
        check_vma=False,
    )
```

time: 152 us -> 74.1 us (0.49)
  waiting for transfers between devices: 67.9 us -> 37.3 us
  matrix products: 36.1 us -> 5.82 us
  blocking collectives: 13.1 us -> 0 us
  local copies, waits for them, and re-layouts: 5.66 us -> 3.03 us
  other arithmetic: 6.68 us -> 4.86 us
  starting transfers between devices: 20.4 us -> 22 us
    all_to_all x2, waiting for transfers between devices: 57.5 us -> 19.7 us  [the longest x1 14.2 us: look_up(): lax.all_to_all(jnp.broadcast_to(next_token[None, :], (devices, hyp_rows))...]
    dot_general x16 -> x2, matrix products: 31 us -> 0.45 us  [the longest x1 0.26 us: look_up(): jnp.dot(onehot, proj_table.reshape(vocab_rows, width), preferred_element_...]
    unnamed x1 -> x0, blocking collectives: 13.1 us -> none
    ppermute x7 -> x9, waiting for transfers between devices: 10.4 us -> 17.5 us  [swap(): return lax.ppermute(block, 'beam', route)]
    another operation x16 -> x0, other arithmetic: 2.59 us -> none
    unnamed x23 -> x15, local copies, waits for them, and re-layouts: 3.69 us -> 1.38 us
    sub x2 -> x1, other arithmetic: 2.35 us -> 0.76 us  [advance(): state_now - strengths[:, reflect, :, None, None] * (applied - value_row)[...]
    ppermute x7 -> x9, starting transfers between devices: 11.3 us -> 12.3 us  [swap(): return lax.ppermute(block, 'beam', route)]
  transfers between devices with their start and end apart: 9 -> 11, of which waited for: 3 -> 6; matrix products, arithmetic and copies ran while one was open for 19% -> 4% of each run, Pallas kernels for 0% -> 0%
where the time goes in v1:
time: 74.1 us; the launch traced here: 73.8 us
  waiting for transfers between devices  37.3 us (50%)
  starting transfers between devices  22 us (30%)
  matrix products  5.82 us (8%)
  other arithmetic  4.86 us (7%)
  local copies, waits for them, and re-layouts  3.03 us (4%)
  between operations  0.84 us (1%)
    ppermute x9, waiting for transfers between devices, swap(): return lax.ppermute(block, 'beam', route)  17.5 us
    all_to_all x1, waiting for transfers between devices, look_up(): lax.all_to_all(jnp.broadcast_to(next_token[None, :], (devices, hyp_rows))...  14.2 us
    ppermute x9, starting transfers between devices, swap(): return lax.ppermute(block, 'beam', route)  12.3 us
    all_to_all x1, waiting for transfers between devices, look_up(): lax.all_to_all(rows, 'beam', split_axis=0, concat_axis=0, tiled=True)  5.57 us
    all_to_all x1, starting transfers between devices, look_up(): lax.all_to_all(rows, 'beam', split_axis=0, concat_axis=0, tiled=True)  4.86 us
    all_to_all x1, starting transfers between devices, look_up(): lax.all_to_all(jnp.broadcast_to(next_token[None, :], (devices, hyp_rows))...  4.79 us
    dot_general x2, matrix products, advance(): jnp.einsum('nhvd,nhd->nhv', state_now, key_unit, precision=lax.Precision....  3.65 us
    dot_general x1, matrix products, advance(): jnp.einsum('nhvd,nhd->nhv', state_now, query_unit, precision=lax.Precisio...  1.72 us
  transfers between devices with their start and end apart: 11, of which 6 were waited for; matrix products, arithmetic and copies ran while one was open for 4% of the time, Pallas kernels for 0%

profile of v1, /device:TPU:0, one launch (start us, length us, event | category | flops | bytes accessed | tf_op | source)
XLA Modules:
  0.0 73.8 jit_solution(15359095404907964632)
XLA Ops:
  0.6 1.4 %slice_convert_fusion.1 = (f16[4,2,128,128]{3,2,1,0:T(8,128)(2,1)S(1)}, f16[4,2,128,128]{3,2,1,0:T(8,128)(2,1)S(1)}) fusion(f32[4,4,128,128]{3,2,1,0:T(8,128)} %param.6), kind=kLoop, calls=%fused_computation.14 | loop fusion | flops 262144 | bytes 1572864 | tf_op jit(solution)/shard_map/convert_element_type | solution.py:94
  2.0 4.1 %collective-permute-start.1 = (f16[4,2,128,128]{3,2,1,0:T(8,128)(2,1)S(1)}, f16[4,2,128,128]{3,2,1,0:T(8,128)(2,1)S(1)}, u32[]{:S(2)}, u32[]{:S(2)}) collective-permute-start(f16[4,2,128,128]{3,2,1,0:T(8,128)(2,1)S(1)} %get-tuple-element.4), channel_id=1, source_target_pairs={{0,8},{2,10},{4,12},{6,14},{8,0},{10,2},{12,4},{14,6},{1,9},{3,11}... | collective-permute-start | bytes 786440 | tf_op jit(solution)/shard_map/ppermute | solution.py:17
  6.2 1.5 %collective-permute-start.3 = (f16[4,2,128,128]{3,2,1,0:T(8,128)(2,1)S(1)}, f16[4,2,128,128]{3,2,1,0:T(8,128)(2,1)S(1)}, u32[]{:S(2)}, u32[]{:S(2)}) collective-permute-start(f16[4,2,128,128]{3,2,1,0:T(8,128)(2,1)S(1)} %get-tuple-element.4), channel_id=1, source_target_pairs={{0,2},{2,0},{4,6},{6,4},{8,10},{10,8},{12,14},{14,12},{1,3},{3,1},... | collective-permute-start | bytes 786440 | tf_op jit(solution)/shard_map/ppermute | solution.py:17
  7.7 0.3 collective-permute-start.5
  8.0 0.3 collective-permute-start.7
  8.3 1.8 %collective-permute-start = (s32[4]{0:T(128)S(1)}, s32[4]{0:T(128)S(1)}, u32[]{:S(2)}, u32[]{:S(2)}) collective-permute-start(s32[4]{0:T(128)S(1)} %copy-done.6), channel_id=1, source_target_pairs={{0,4},{2,6},{4,0},{6,2},{8,12},{10,14},{12,8},{14,10},{1,5},{3,7},... | collective-permute-start | bytes 56 | tf_op jit(solution)/shard_map/ppermute | solution.py:17
  10.1 0.6 broadcast_in_dim.82
  10.7 4.8 %all-to-all-start = ((s32[8,1,4]{2,1,0:T(1,128)}), s32[8,1,4]{2,1,0:T(1,128)S(1)}, u32[]{:S(2)}, u32[]{:S(2)}) async-start(s32[8,1,4]{2,1,0:T(1,128)} %broadcast_in_dim.82), calls=%async_computation | async-start | bytes 8192 | tf_op jit(solution)/shard_map/all_to_all | solution.py:52
  15.6 0.6 copy-done.3
  16.2 14.2 %all-to-all-done = s32[8,1,4]{2,1,0:T(1,128)S(1)} async-done(((s32[8,1,4]{2,1,0:T(1,128)}), s32[8,1,4]{2,1,0:T(1,128)S(1)}, u32[]{:S(2)}, u32[]{:S(2)}) %all-to-all-start) | async-done | bytes 160 | tf_op jit(solution)/shard_map/all_to_all | solution.py:52
  30.5 0.3 convolution_convert_fusion
  30.8 0.2 convolution_convert_fusion.1
  30.9 0.1 copy.15
  31.1 0.7 reshape.101
  31.8 4.9 %all-to-all-start.1 = ((bf16[8,4,2572]{2,1,0:T(4,128)(2,1)}), bf16[8,4,2572]{2,1,0:T(4,128)(2,1)S(1)}, u32[]{:S(2)}, u32[]{:S(2)}) async-start(bf16[8,4,2572]{2,1,0:T(4,128)(2,1)} %reshape.101), calls=%async_computation.1 | async-start | bytes 344064 | tf_op jit(solution)/shard_map/all_to_all | solution.py:67
  36.7 2.1 %collective-permute-start.2 = (f16[4,2,128,128]{3,2,1,0:T(8,128)(2,1)S(1)}, f16[4,2,128,128]{3,2,1,0:T(8,128)(2,1)S(1)}, u32[]{:S(2)}, u32[]{:S(2)}) collective-permute-start(f16[4,2,128,128]{3,2,1,0:T(8,128)(2,1)S(1)} %collective-permute-done.1), channel_id=1, source_target_pairs={{0,2},{2,0},{4,6},{6,4},{8,10},{10,8},{12,14},{14,12},{1,3},{3,1},... | collective-permute-start | bytes 786440 | tf_op jit(solution)/shard_map/ppermute | solution.py:17
  38.9 5.6 %all-to-all-done.1 = bf16[8,4,2572]{2,1,0:T(4,128)(2,1)S(1)} async-done(((bf16[8,4,2572]{2,1,0:T(4,128)(2,1)}), bf16[8,4,2572]{2,1,0:T(4,128)(2,1)S(1)}, u32[]{:S(2)}, u32[]{:S(2)}) %all-to-all-start.1) | async-done | bytes 164640 | tf_op jit(solution)/shard_map/all_to_all | solution.py:67
  45.0 0.1 fusion.17
  45.3 2.5 %collective-permute-done.2 = f16[4,2,128,128]{3,2,1,0:T(8,128)(2,1)S(1)} collective-permute-done((f16[4,2,128,128]{3,2,1,0:T(8,128)(2,1)S(1)}, f16[4,2,128,128]{3,2,1,0:T(8,128)(2,1)S(1)}, u32[]{:S(2)}, u32[]{:S(2)}) %collective-permute-start.2) | collective-permute-done | bytes 262176 | tf_op jit(solution)/shard_map/ppermute | solution.py:17
  47.8 4.4 %collective-permute-done.6 = f16[4,2,128,128]{3,2,1,0:T(8,128)(2,1)S(1)} collective-permute-done((f16[4,2,128,128]{3,2,1,0:T(8,128)(2,1)S(1)}, f16[4,2,128,128]{3,2,1,0:T(8,128)(2,1)S(1)}, u32[]{:S(2)}, u32[]{:S(2)}) %collective-permute-start.6) | collective-permute-done | bytes 262176 | tf_op jit(solution)/shard_map/ppermute | solution.py:17
  52.2 0.5 select_select_fusion.3
  52.7 1.5 %collective-permute-start.4 = (f16[4,2,128,128]{3,2,1,0:T(8,128)(2,1)S(1)}, f16[4,2,128,128]{3,2,1,0:T(8,128)(2,1)S(1)}, u32[]{:S(2)}, u32[]{:S(2)}) collective-permute-start(f16[4,2,128,128]{3,2,1,0:T(8,128)(2,1)S(1)} %get-tuple-element.15), channel_id=1, source_target_pairs={{0,4},{2,6},{4,0},{6,2},{8,12},{10,14},{12,8},{14,10},{1,5},{3,7},... | collective-permute-start | bytes 786440 | tf_op jit(solution)/shard_map/ppermute | solution.py:17
  54.2 0.6 collective-permute-start.8
  54.9 7.1 %collective-permute-done.4 = f16[4,2,128,128]{3,2,1,0:T(8,128)(2,1)S(1)} collective-permute-done((f16[4,2,128,128]{3,2,1,0:T(8,128)(2,1)S(1)}, f16[4,2,128,128]{3,2,1,0:T(8,128)(2,1)S(1)}, u32[]{:S(2)}, u32[]{:S(2)}) %collective-permute-start.4) | collective-permute-done | bytes 262176 | tf_op jit(solution)/shard_map/ppermute | solution.py:17
  62.0 3.5 %collective-permute-done.8 = f16[4,2,128,128]{3,2,1,0:T(8,128)(2,1)S(1)} collective-permute-done((f16[4,2,128,128]{3,2,1,0:T(8,128)(2,1)S(1)}, f16[4,2,128,128]{3,2,1,0:T(8,128)(2,1)S(1)}, u32[]{:S(2)}, u32[]{:S(2)}) %collective-permute-start.8) | collective-permute-done | bytes 262176 | tf_op jit(solution)/shard_map/ppermute | solution.py:17
  65.5 0.5 select_select_fusion.1
  66.0 1.8 %fusion.1 = f32[4,4,1,128]{3,2,1,0:T(1,128)S(1)} fusion(f32[4,4,128,1]{2,3,1,0:T(1,128)S(1)} %bitcast.54, f32[4,2,128,128]{3,2,1,0:T(8,128)S(1)} %get-tuple-element.3, f32[4,2,128,128]{3,2,1,0:T(8,128)S(1)} %get-tuple-element.2, f32[4,4]{1,0:T(4,128)S(1)} %bitcast.51), kind=kOutput, calls=%fused_computation.6 | convolution fusion | flops 3670016 | bytes 1065024 | tf_op jit(solution)/shard_map/nhvd,nhd->nhv/dot_general | solution.py:31
  67.9 1.9 %fusion = f32[4,4,1,128]{3,2,1,0:T(1,128)S(1)} fusion(f32[4,4,128,1]{2,3,1,0:T(1,128)S(1)} %bitcast.55, f32[4,2,128,128]{3,2,1,0:T(8,128)S(1)} %get-tuple-element.3, f32[4,2,128,128]{3,2,1,0:T(8,128)S(1)} %get-tuple-element.2, f32[4,4,128]{2,1,0:T(4,128)S(1)} %bitcast.46, f32[4,4,128]{2,1,0:T(4,128)S(1)} %subtract_multiply_fusion.1, f32[4,4]{1,0:T(4,128)S(1)} %bitcast.52), kind=kOutput, calls=%fused_computation.5 | convolution fusion | flops 4194304 | bytes 1081408 | tf_op jit(solution)/shard_map/nhvd,nhd->nhv/dot_general | solution.py:31
  69.8 0.8 %multiply_subtract_fusion = f32[4,4,128,128]{3,2,1,0:T(8,128)S(1)} fusion(f32[4,2,128,128]{3,2,1,0:T(8,128)S(1)} %get-tuple-element.3, f32[4,2,128,128]{3,2,1,0:T(8,128)S(1)} %get-tuple-element.2, f32[4,4,128]{2,1,0:T(4,128)S(1)} %bitcast.48, f32[4,4,128]{2,1,0:T(4,128)S(1)} %subtract_multiply_fusion, f32[4,4,128]{2,1,0:T(4,128)S(1)} %bitcast.47, ...), kind=kLoop, calls=%fused_computation.3 | loop fusion | flops 1572864 | bytes 2129984 | tf_op jit(solution)/shard_map/sub | solution.py:33
  70.6 1.7 %fusion.20 = f32[4,4,1,128]{3,2,1,0:T(1,128)S(1)} fusion(f32[4,4,128,128]{3,2,1,0:T(8,128)S(1)} %multiply_subtract_fusion, f32[4,4,128,1]{2,3,1,0:T(1,128)S(1)} %bitcast.45), kind=kOutput, calls=%fused_computation.59 | convolution fusion | flops 3145728 | bytes 1064960 | tf_op jit(solution)/shard_map/nhvd,nhd->nhv/dot_general | solution.py:39
  72.4 0.7 copy-done.4
  73.1 0.7 multiply_convert_fusion
  (46 shorter events, 1.4 us)
Async XLA Ops:
  0.6 14.9 %copy-start.2 = (bf16[128,4,640]{2,1,0:T(4,128)(2,1)S(1)}, bf16[128,4,640]{2,1,0:T(4,128)(2,1)}, u32[]{:S(2)}) copy-start(bf16[128,4,640]{2,1,0:T(4,128)(2,1)} %param.9) | copy-start | bytes 1966084
  2.0 6.3 %copy-start.6 = (s32[4]{0:T(128)S(1)}, s32[4]{0:T(128)}, u32[]{:S(2)}) copy-start(s32[4]{0:T(128)} %param.7) | copy-start | bytes 52
  2.0 8.1 %copy-start.5 = (s32[4]{0:T(128)S(1)}, s32[4]{0:T(128)}, u32[]{:S(2)}) copy-start(s32[4]{0:T(128)} %param.8) | copy-start | bytes 52
  2.0 34.7 %collective-permute-start.1 = (f16[4,2,128,128]{3,2,1,0:T(8,128)(2,1)S(1)}, f16[4,2,128,128]{3,2,1,0:T(8,128)(2,1)S(1)}, u32[]{:S(2)}, u32[]{:S(2)}) collective-permute-start(f16[4,2,128,128]{3,2,1,0:T(8,128)(2,1)S(1)} %get-tuple-element.4), channel_id=1, source_target_pairs={{0,8},{2,10},{4,12},{6,14},{8,0},{10,2},{12,4},{14,6},{1,9},{3,11}... | collective-permute-start | bytes 786440 | tf_op jit(solution)/shard_map/ppermute | solution.py:17
  6.2 39.1 %collective-permute-start.3 = (f16[4,2,128,128]{3,2,1,0:T(8,128)(2,1)S(1)}, f16[4,2,128,128]{3,2,1,0:T(8,128)(2,1)S(1)}, u32[]{:S(2)}, u32[]{:S(2)}) collective-permute-start(f16[4,2,128,128]{3,2,1,0:T(8,128)(2,1)S(1)} %get-tuple-element.4), channel_id=1, source_target_pairs={{0,2},{2,0},{4,6},{6,4},{8,10},{10,8},{12,14},{14,12},{1,3},{3,1},... | collective-permute-start | bytes 786440 | tf_op jit(solution)/shard_map/ppermute | solution.py:17
  7.7 31.1 %collective-permute-start.5 = (f16[4,2,128,128]{3,2,1,0:T(8,128)(2,1)S(1)}, f16[4,2,128,128]{3,2,1,0:T(8,128)(2,1)S(1)}, u32[]{:S(2)}, u32[]{:S(2)}) collective-permute-start(f16[4,2,128,128]{3,2,1,0:T(8,128)(2,1)S(1)} %get-tuple-element.5), channel_id=1, source_target_pairs={{0,8},{2,10},{4,12},{6,14},{8,0},{10,2},{12,4},{14,6},{1,9},{3,11}... | collective-permute-start | bytes 786440 | tf_op jit(solution)/shard_map/ppermute | solution.py:17
  8.0 37.3 %collective-permute-start.7 = (f16[4,2,128,128]{3,2,1,0:T(8,128)(2,1)S(1)}, f16[4,2,128,128]{3,2,1,0:T(8,128)(2,1)S(1)}, u32[]{:S(2)}, u32[]{:S(2)}) collective-permute-start(f16[4,2,128,128]{3,2,1,0:T(8,128)(2,1)S(1)} %get-tuple-element.5), channel_id=1, source_target_pairs={{0,2},{2,0},{4,6},{6,4},{8,10},{10,8},{12,14},{14,12},{1,3},{3,1},... | collective-permute-start | bytes 786440 | tf_op jit(solution)/shard_map/ppermute | solution.py:17
  8.3 28.4 %collective-permute-start = (s32[4]{0:T(128)S(1)}, s32[4]{0:T(128)S(1)}, u32[]{:S(2)}, u32[]{:S(2)}) collective-permute-start(s32[4]{0:T(128)S(1)} %copy-done.6), channel_id=1, source_target_pairs={{0,4},{2,6},{4,0},{6,2},{8,12},{10,14},{12,8},{14,10},{1,5},{3,7},... | collective-permute-start | bytes 56 | tf_op jit(solution)/shard_map/ppermute | solution.py:17
  10.7 19.7 %all-to-all-start = ((s32[8,1,4]{2,1,0:T(1,128)}), s32[8,1,4]{2,1,0:T(1,128)S(1)}, u32[]{:S(2)}, u32[]{:S(2)}) async-start(s32[8,1,4]{2,1,0:T(1,128)} %broadcast_in_dim.82), calls=%async_computation | async-start | bytes 8192 | tf_op jit(solution)/shard_map/all_to_all | solution.py:52
  15.5 0.7 copy-start.3
  31.8 12.7 %all-to-all-start.1 = ((bf16[8,4,2572]{2,1,0:T(4,128)(2,1)}), bf16[8,4,2572]{2,1,0:T(4,128)(2,1)S(1)}, u32[]{:S(2)}, u32[]{:S(2)}) async-start(bf16[8,4,2572]{2,1,0:T(4,128)(2,1)} %reshape.101), calls=%async_computation.1 | async-start | bytes 344064 | tf_op jit(solution)/shard_map/all_to_all | solution.py:67
  36.7 11.1 %collective-permute-start.2 = (f16[4,2,128,128]{3,2,1,0:T(8,128)(2,1)S(1)}, f16[4,2,128,128]{3,2,1,0:T(8,128)(2,1)S(1)}, u32[]{:S(2)}, u32[]{:S(2)}) collective-permute-start(f16[4,2,128,128]{3,2,1,0:T(8,128)(2,1)S(1)} %collective-permute-done.1), channel_id=1, source_target_pairs={{0,2},{2,0},{4,6},{6,4},{8,10},{10,8},{12,14},{14,12},{1,3},{3,1},... | collective-permute-start | bytes 786440 | tf_op jit(solution)/shard_map/ppermute | solution.py:17
  38.8 13.4 %collective-permute-start.6 = (f16[4,2,128,128]{3,2,1,0:T(8,128)(2,1)S(1)}, f16[4,2,128,128]{3,2,1,0:T(8,128)(2,1)S(1)}, u32[]{:S(2)}, u32[]{:S(2)}) collective-permute-start(f16[4,2,128,128]{3,2,1,0:T(8,128)(2,1)S(1)} %collective-permute-done.5), channel_id=1, source_target_pairs={{0,2},{2,0},{4,6},{6,4},{8,10},{10,8},{12,14},{14,12},{1,3},{3,1},... | collective-permute-start | bytes 786440 | tf_op jit(solution)/shard_map/ppermute | solution.py:17
  52.2 13.3 %copy-start = (f32[4,4,128,128]{3,2,1,0:T(8,128)S(1)}, f32[4,4,128,128]{3,2,1,0:T(8,128)}, u32[]{:S(2)}) copy-start(f32[4,4,128,128]{3,2,1,0:T(8,128)} %param.6) | copy-start | bytes 3145732
  52.7 9.2 %collective-permute-start.4 = (f16[4,2,128,128]{3,2,1,0:T(8,128)(2,1)S(1)}, f16[4,2,128,128]{3,2,1,0:T(8,128)(2,1)S(1)}, u32[]{:S(2)}, u32[]{:S(2)}) collective-permute-start(f16[4,2,128,128]{3,2,1,0:T(8,128)(2,1)S(1)} %get-tuple-element.15), channel_id=1, source_target_pairs={{0,4},{2,6},{4,0},{6,2},{8,12},{10,14},{12,8},{14,10},{1,5},{3,7},... | collective-permute-start | bytes 786440 | tf_op jit(solution)/shard_map/ppermute | solution.py:17
  54.2 11.2 %collective-permute-start.8 = (f16[4,2,128,128]{3,2,1,0:T(8,128)(2,1)S(1)}, f16[4,2,128,128]{3,2,1,0:T(8,128)(2,1)S(1)}, u32[]{:S(2)}, u32[]{:S(2)}) collective-permute-start(f16[4,2,128,128]{3,2,1,0:T(8,128)(2,1)S(1)} %get-tuple-element.16), channel_id=1, source_target_pairs={{0,4},{2,6},{4,0},{6,2},{8,12},{10,14},{12,8},{14,10},{1,5},{3,7},... | collective-permute-start | bytes 786440 | tf_op jit(solution)/shard_map/ppermute | solution.py:17
  70.6 3.2 %copy-start.1 = (f32[4,4,128,128]{3,2,1,0:T(8,128)}, f32[4,4,128,128]{3,2,1,0:T(8,128)S(1)}, u32[]{:S(2)}) copy-start(f32[4,4,128,128]{3,2,1,0:T(8,128)S(1)} %multiply_subtract_fusion) | copy-start | bytes 3145732
  72.4 0.7 copy-start.4

commit v2 on v1

v2 whole, which is shorter than its diff:
```python
import jax
import jax.numpy as jnp
from jax import lax
from jax.experimental import pallas as pl
from jax.sharding import PartitionSpec as P

HEAD_DIM = 128
BEAMS = 8
FAR, NEAR, SIDE = 4, 2, 1
WIRE = jnp.float16
PARTS = (2, 2)


def swap(block, mask):
    devices = lax.axis_size("beam")
    spacing = devices // BEAMS
    route = [(i, ((i // spacing) ^ mask) * spacing + i % spacing) for i in range(devices)]
    return lax.ppermute(block, "beam", route)


def exchange(block):
    return lax.all_to_all(block, "beam", split_axis=0, concat_axis=0, tiled=True)


def unit_norm(vector):
    return vector * lax.rsqrt(jnp.sum(vector * vector, axis=-1, keepdims=True) + 1e-06)


def pack_vectors(entries, gate_entries):
    units = unit_norm(entries[:, :, :3, :])
    gates = jnp.swapaxes(jax.nn.sigmoid(gate_entries), 1, 2)
    gates = gates * jnp.array([1.0, 2.0, 2.0], jnp.float32)
    gates = jnp.broadcast_to(gates[:, :, :, None], gates.shape + (HEAD_DIM,))
    return jnp.concatenate([units, entries[:, :, 3:, :], gates], axis=2)


def next_head(refs, row, head):
    for ref in refs:
        if head < ref.shape[1]:
            return ref[row, head]
        head -= ref.shape[1]


def column_sum(block):
    return jnp.sum(block, axis=1, keepdims=True)


def advance_body(*refs):
    vectors_ref, gain_ref, *parent_refs, readout_ref, states_ref = refs
    rows, heads = states_ref.shape[:2]
    shape = (HEAD_DIM, HEAD_DIM)
    diagonal = lax.broadcasted_iota(jnp.int32, shape, 0) == lax.broadcasted_iota(jnp.int32, shape, 1)
    for row in range(rows):
        outs = []
        for head in range(heads):
            vecs = vectors_ref[row, head]
            parent = next_head(parent_refs, row, head)
            query, key1, key2 = vecs[0:1], vecs[1:2], vecs[2:3]
            value1, value2 = vecs[3:4], vecs[4:5]
            beta1, beta2 = vecs[6:7, 0:1], vecs[7:8, 0:1]
            state = vecs[5:6] * parent
            part = state * key1
            step1 = beta1 * column_sum(jnp.where(diagonal, part - value1, part))
            state = state - step1 * key1
            part = state * key2
            step2 = beta2 * column_sum(jnp.where(diagonal, part - value2, part))
            state = state - step2 * key2
            states_ref[row, head] = state
            out = column_sum(state * query)
            outs.append(jnp.sum(jnp.where(diagonal, out, 0.0), axis=0, keepdims=True))
        out = jnp.concatenate(outs, axis=0)
        scale = lax.rsqrt(jnp.mean(out * out, axis=1, keepdims=True) + 1e-05)
        readout_ref[row] = (gain_ref[...] * out * scale).astype(readout_ref.dtype)


def advance(parents, entries, gate_entries, gain):
    rows = parents[0].shape[0]
    heads = gain.shape[0]
    return pl.pallas_call(
        advance_body,
        out_shape=(
            jax.ShapeDtypeStruct((rows, heads, HEAD_DIM), jnp.bfloat16),
            jax.ShapeDtypeStruct((rows, heads, HEAD_DIM, HEAD_DIM), jnp.float32),
        ),
        name="advance",
    )(pack_vectors(entries, gate_entries), gain, *parents)


def look_up(next_token, proj_table, gate_table):
    hyp_rows = next_token.shape[0]
    devices = lax.axis_size("beam")
    vocab_rows, head_count = proj_table.shape[:2]
    tokens = exchange(
        jnp.broadcast_to(next_token[None, :], (devices, hyp_rows))
    ).reshape(devices * hyp_rows)
    local_ids = tokens - lax.axis_index("beam") * vocab_rows
    onehot = (local_ids[:, None] == jnp.arange(vocab_rows, dtype=jnp.int32)[None, :]).astype(
        jnp.bfloat16
    )
    width = head_count * 5 * HEAD_DIM
    looked = jnp.dot(
        onehot, proj_table.reshape(vocab_rows, width), preferred_element_type=jnp.float32
    ).astype(jnp.bfloat16)
    looked_gates = jnp.dot(
        onehot, gate_table.reshape(vocab_rows, 3 * head_count), preferred_element_type=jnp.float32
    ).astype(jnp.bfloat16)
    rows = jnp.concatenate([looked, looked_gates], axis=1).reshape(devices, hyp_rows, -1)
    arrived = exchange(rows)
    summed = jnp.sum(arrived, axis=0, dtype=jnp.float32)
    entries = summed[:, :width].reshape(hyp_rows, head_count, 5, HEAD_DIM)
    gate_entries = summed[:, width:].reshape(hyp_rows, 3, head_count)
    return entries, gate_entries


def pick(near, far, far_side, side, relation):
    rel = relation[:, None, None, None]
    return jnp.where(
        (rel & FAR) != 0,
        jnp.where((rel & SIDE) != 0, far_side, far),
        jnp.where((rel & SIDE) != 0, side, near),
    )


def step(states, parent_beam, next_token, proj_table, gate_table, gain):
    devices = lax.axis_size("beam")
    my_beam = lax.axis_index("beam") // (devices // BEAMS)
    relation = parent_beam ^ my_beam
    peer_relation = swap(parent_beam, NEAR) ^ my_beam
    entries, gate_entries = look_up(next_token, proj_table, gate_table)
    head_count = states.shape[1]
    unit = head_count // sum(PARTS)
    crossed = (relation & NEAR)[:, None, None, None] != 0
    parents = []
    start = 0
    for part in PARTS:
        exact = states[:, start : start + part * unit]
        start += part * unit
        near = exact.astype(WIRE)
        far = swap(near, FAR)
        side = swap(near, SIDE)
        far_side = swap(far, SIDE)
        block = swap(pick(near, far, far_side, side, peer_relation), NEAR)
        mine = pick(
            exact,
            far.astype(jnp.float32),
            far_side.astype(jnp.float32),
            side.astype(jnp.float32),
            relation,
        )
        parents.append(jnp.where(crossed, block.astype(jnp.float32), mine))
    return advance(parents, entries, gate_entries, gain)


def solution(mesh):
    return jax.shard_map(
        step,
        mesh=mesh,
        in_specs=(
            P(("groups", "beam"), "mp", None, None),
            P(("groups", "beam")),
            P(("groups", "beam")),
            P("beam", "mp", None),
            P("beam", None, "mp"),
            P("mp", None),
        ),
        out_specs=(P(("groups", "beam"), "mp", None), P(("groups", "beam"), "mp", None, None)),
        check_vma=False,
    )
```

time: 74.1 us -> 75.2 us (1.015)
  Pallas kernels: 0 us -> 7.83 us
  matrix products: 5.82 us -> 0.45 us
  waiting for transfers between devices: 37.3 us -> 36.2 us
    pallas_call x0 -> x1, Pallas kernels: none -> 7.83 us  [advance(): pl.pallas_call(advance_body, out_shape=(jax.ShapeDtypeStruct((rows, heads...]
    dot_general x3 -> x0, matrix products: 5.37 us -> none  [the longest x2 3.65 us: advance(): jnp.einsum('nhvd,nhd->nhv', state_now, key_unit, precision=lax.Precision....]
    ppermute x9, waiting for transfers between devices: 17.5 us -> 16.5 us  [swap(): return lax.ppermute(block, 'beam', route)]
    select_n x1, other arithmetic: 0.54 us -> 1.52 us  [step(): parents.append(jnp.where(crossed, block.astype(jnp.float32), mine))]
    sub x1 -> x0, other arithmetic: 0.76 us -> none  [advance(): state_now - strengths[:, reflect, :, None, None] * (applied - value_row)[...]
    convert_element_type x2 -> x1, other arithmetic: 2.04 us -> 1.37 us  [step(): near = exact.astype(WIRE)]
  transfers between devices with their start and end apart: 11 -> 11, of which waited for: 6 -> 6; matrix products, arithmetic and copies ran while one was open for 4% -> 5% of each run, Pallas kernels for 0% -> 0%
where the time goes in v2:
time: 75.2 us; the launch traced here: 74.9 us
  waiting for transfers between devices  36.2 us (48%)
  starting transfers between devices  22 us (29%)
  Pallas kernels  7.83 us (10%)
  other arithmetic  4.47 us (6%)
  local copies, waits for them, and re-layouts  3.08 us (4%)
  between operations  0.81 us (1%)
    all_to_all x2, waiting for transfers between devices, exchange(): lax.all_to_all(block, 'beam', split_axis=0, concat_axis=0, tiled=True)  19.7 us
    ppermute x9, waiting for transfers between devices, swap(): return lax.ppermute(block, 'beam', route)  16.5 us
    ppermute x9, starting transfers between devices, swap(): return lax.ppermute(block, 'beam', route)  12.3 us
    all_to_all x2, starting transfers between devices, exchange(): lax.all_to_all(block, 'beam', split_axis=0, concat_axis=0, tiled=True)  9.66 us
    pallas_call x1, Pallas kernels, advance(): pl.pallas_call(advance_body, out_shape=(jax.ShapeDtypeStruct((rows, heads...  7.83 us
    select_n x1, other arithmetic, step(): parents.append(jnp.where(crossed, block.astype(jnp.float32), mine))  1.52 us
  transfers between devices with their start and end apart: 11, of which 6 were waited for; matrix products, arithmetic and copies ran while one was open for 5% of the time, Pallas kernels for 0%

profile of v2, /device:TPU:0, one launch (start us, length us, event | category | flops | bytes accessed | tf_op | source)
XLA Modules:
  0.0 74.9 jit_solution(7655484655641157098)
XLA Ops:
  0.6 1.4 %slice_convert_fusion = (f16[4,2,128,128]{3,2,1,0:T(8,128)(2,1)S(1)}, f16[4,2,128,128]{3,2,1,0:T(8,128)(2,1)S(1)}) fusion(f32[4,4,128,128]{3,2,1,0:T(8,128)} %param.7), kind=kLoop, calls=%fused_computation.4 | loop fusion | flops 262144 | bytes 1572864 | tf_op jit(solution)/shard_map/convert_element_type | solution.py:138
  2.0 4.1 %collective-permute-start.1 = (f16[4,2,128,128]{3,2,1,0:T(8,128)(2,1)S(1)}, f16[4,2,128,128]{3,2,1,0:T(8,128)(2,1)S(1)}, u32[]{:S(2)}, u32[]{:S(2)}) collective-permute-start(f16[4,2,128,128]{3,2,1,0:T(8,128)(2,1)S(1)} %get-tuple-element.5), channel_id=1, source_target_pairs={{0,8},{2,10},{4,12},{6,14},{8,0},{10,2},{12,4},{14,6},{1,9},{3,11}... | collective-permute-start | bytes 786440 | tf_op jit(solution)/shard_map/ppermute | solution.py:18
  6.2 1.5 %collective-permute-start.3 = (f16[4,2,128,128]{3,2,1,0:T(8,128)(2,1)S(1)}, f16[4,2,128,128]{3,2,1,0:T(8,128)(2,1)S(1)}, u32[]{:S(2)}, u32[]{:S(2)}) collective-permute-start(f16[4,2,128,128]{3,2,1,0:T(8,128)(2,1)S(1)} %get-tuple-element.5), channel_id=1, source_target_pairs={{0,2},{2,0},{4,6},{6,4},{8,10},{10,8},{12,14},{14,12},{1,3},{3,1},... | collective-permute-start | bytes 786440 | tf_op jit(solution)/shard_map/ppermute | solution.py:18
  7.7 0.3 collective-permute-start.5
  8.0 0.3 collective-permute-start.7
  8.3 1.8 %collective-permute-start = (s32[4]{0:T(128)S(1)}, s32[4]{0:T(128)S(1)}, u32[]{:S(2)}, u32[]{:S(2)}) collective-permute-start(s32[4]{0:T(128)S(1)} %copy-done.4), channel_id=1, source_target_pairs={{0,4},{2,6},{4,0},{6,2},{8,12},{10,14},{12,8},{14,10},{1,5},{3,7},... | collective-permute-start | bytes 56 | tf_op jit(solution)/shard_map/ppermute | solution.py:18
  10.1 0.6 broadcast_in_dim.79
  10.7 4.8 %all-to-all-start = ((s32[8,1,4]{2,1,0:T(1,128)}), s32[8,1,4]{2,1,0:T(1,128)S(1)}, u32[]{:S(2)}, u32[]{:S(2)}) async-start(s32[8,1,4]{2,1,0:T(1,128)} %broadcast_in_dim.79), calls=%async_computation | async-start | bytes 8192 | tf_op jit(solution)/shard_map/all_to_all | solution.py:22
  15.6 0.6 copy-done.2
  16.2 14.2 %all-to-all-done = s32[8,1,4]{2,1,0:T(1,128)S(1)} async-done(((s32[8,1,4]{2,1,0:T(1,128)}), s32[8,1,4]{2,1,0:T(1,128)S(1)}, u32[]{:S(2)}, u32[]{:S(2)}) %all-to-all-start) | async-done | bytes 160 | tf_op jit(solution)/shard_map/all_to_all | solution.py:22
  30.5 0.3 convolution_convert_fusion
  30.8 0.2 convolution_convert_fusion.1
  30.9 0.1 copy.15
  31.1 0.7 reshape.62
  31.8 4.9 %all-to-all-start.1 = ((bf16[8,4,2572]{2,1,0:T(4,128)(2,1)}), bf16[8,4,2572]{2,1,0:T(4,128)(2,1)S(1)}, u32[]{:S(2)}, u32[]{:S(2)}) async-start(bf16[8,4,2572]{2,1,0:T(4,128)(2,1)} %reshape.62), calls=%async_computation.1 | async-start | bytes 344064 | tf_op jit(solution)/shard_map/all_to_all | solution.py:22
  36.7 2.1 %collective-permute-start.2 = (f16[4,2,128,128]{3,2,1,0:T(8,128)(2,1)S(1)}, f16[4,2,128,128]{3,2,1,0:T(8,128)(2,1)S(1)}, u32[]{:S(2)}, u32[]{:S(2)}) collective-permute-start(f16[4,2,128,128]{3,2,1,0:T(8,128)(2,1)S(1)} %collective-permute-done.1), channel_id=1, source_target_pairs={{0,2},{2,0},{4,6},{6,4},{8,10},{10,8},{12,14},{14,12},{1,3},{3,1},... | collective-permute-start | bytes 786440 | tf_op jit(solution)/shard_map/ppermute | solution.py:18
  38.8 0.1 collective-permute-start.6
  38.9 5.6 %all-to-all-done.1 = bf16[8,4,2572]{2,1,0:T(4,128)(2,1)S(1)} async-done(((bf16[8,4,2572]{2,1,0:T(4,128)(2,1)}), bf16[8,4,2572]{2,1,0:T(4,128)(2,1)S(1)}, u32[]{:S(2)}, u32[]{:S(2)}) %all-to-all-start.1) | async-done | bytes 164640 | tf_op jit(solution)/shard_map/all_to_all | solution.py:22
  44.6 0.1 div.9
  44.7 0.6 copy-done.5
  45.3 0.1 multiply_reduce_fusion
  45.5 0.1 copy.16
  45.6 2.2 %collective-permute-done.2 = f16[4,2,128,128]{3,2,1,0:T(8,128)(2,1)S(1)} collective-permute-done((f16[4,2,128,128]{3,2,1,0:T(8,128)(2,1)S(1)}, f16[4,2,128,128]{3,2,1,0:T(8,128)(2,1)S(1)}, u32[]{:S(2)}, u32[]{:S(2)}) %collective-permute-start.2) | collective-permute-done | bytes 262176 | tf_op jit(solution)/shard_map/ppermute | solution.py:18
  47.8 4.4 %collective-permute-done.6 = f16[4,2,128,128]{3,2,1,0:T(8,128)(2,1)S(1)} collective-permute-done((f16[4,2,128,128]{3,2,1,0:T(8,128)(2,1)S(1)}, f16[4,2,128,128]{3,2,1,0:T(8,128)(2,1)S(1)}, u32[]{:S(2)}, u32[]{:S(2)}) %collective-permute-start.6) | collective-permute-done | bytes 262176 | tf_op jit(solution)/shard_map/ppermute | solution.py:18
  52.2 0.5 select_select_fusion.2
  52.7 1.5 %collective-permute-start.4 = (f16[4,2,128,128]{3,2,1,0:T(8,128)(2,1)S(1)}, f16[4,2,128,128]{3,2,1,0:T(8,128)(2,1)S(1)}, u32[]{:S(2)}, u32[]{:S(2)}) collective-permute-start(f16[4,2,128,128]{3,2,1,0:T(8,128)(2,1)S(1)} %get-tuple-element.7), channel_id=1, source_target_pairs={{0,4},{2,6},{4,0},{6,2},{8,12},{10,14},{12,8},{14,10},{1,5},{3,7},... | collective-permute-start | bytes 786440 | tf_op jit(solution)/shard_map/ppermute | solution.py:18
  54.3 0.6 collective-permute-start.8
  55.0 0.6 pad_maximum_fusion.1.refs_0_
  55.6 6.3 %collective-permute-done.4 = f16[4,2,128,128]{3,2,1,0:T(8,128)(2,1)S(1)} collective-permute-done((f16[4,2,128,128]{3,2,1,0:T(8,128)(2,1)S(1)}, f16[4,2,128,128]{3,2,1,0:T(8,128)(2,1)S(1)}, u32[]{:S(2)}, u32[]{:S(2)}) %collective-permute-start.4) | collective-permute-done | bytes 262176 | tf_op jit(solution)/shard_map/ppermute | solution.py:18
  62.0 3.5 %collective-permute-done.8 = f16[4,2,128,128]{3,2,1,0:T(8,128)(2,1)S(1)} collective-permute-done((f16[4,2,128,128]{3,2,1,0:T(8,128)(2,1)S(1)}, f16[4,2,128,128]{3,2,1,0:T(8,128)(2,1)S(1)}, u32[]{:S(2)}, u32[]{:S(2)}) %collective-permute-start.8) | collective-permute-done | bytes 262176 | tf_op jit(solution)/shard_map/ppermute | solution.py:18
  65.5 1.5 %select_select_fusion = (f32[4,2,128,128]{3,2,1,0:T(8,128)}, f32[4,2,128,128]{3,2,1,0:T(8,128)}) fusion(f16[4,2,128,128]{3,2,1,0:T(8,128)(2,1)S(1)} %collective-permute-done.7, f16[4,2,128,128]{3,2,1,0:T(8,128)(2,1)S(1)} %collective-permute-done.5, f16[4,2,128,128]{3,2,1,0:T(8,128)(2,1)S(1)} %collective-permute-done.6, ...), kind=kLoop, calls=%fused_computation.2 | loop fusion | flops 2097152 | bytes 4194316 | tf_op jit(solution)/shard_map/jit(_where)/select_n | solution.py:150
  67.0 7.8 %advance.1 = (bf16[4,4,128]{2,1,0:T(4,128)(2,1)}, f32[4,4,128,128]{3,2,1,0:T(8,128)}) custom-call(f32[4,4,8,128]{3,2,1,0:T(8,128)} %pad_maximum_fusion.1.refs_0_, f32[4,128]{1,0:T(4,128)} %refs_1_.1, f32[4,2,128,128]{3,2,1,0:T(8,128)} %get-tuple-element.3.refs_2_, f32[4,2,128,128]{3,2,1,0:T(8,128)} %get-tuple-element.2.refs_3_), custom_call_target="tpu_custom_call" | custom-call | tf_op jit(solution)/shard_map/advance/pallas_call | solution.py:79
  (31 shorter events, 0.6 us)
Async XLA Ops:
  0.6 14.9 %copy-start.1 = (bf16[128,4,640]{2,1,0:T(4,128)(2,1)S(1)}, bf16[128,4,640]{2,1,0:T(4,128)(2,1)}, u32[]{:S(2)}) copy-start(bf16[128,4,640]{2,1,0:T(4,128)(2,1)} %param.10) | copy-start | bytes 1966084
  2.0 6.3 %copy-start.4 = (s32[4]{0:T(128)S(1)}, s32[4]{0:T(128)}, u32[]{:S(2)}) copy-start(s32[4]{0:T(128)} %param.8) | copy-start | bytes 52
  2.0 8.1 %copy-start.3 = (s32[4]{0:T(128)S(1)}, s32[4]{0:T(128)}, u32[]{:S(2)}) copy-start(s32[4]{0:T(128)} %param.9) | copy-start | bytes 52
  2.0 34.7 %collective-permute-start.1 = (f16[4,2,128,128]{3,2,1,0:T(8,128)(2,1)S(1)}, f16[4,2,128,128]{3,2,1,0:T(8,128)(2,1)S(1)}, u32[]{:S(2)}, u32[]{:S(2)}) collective-permute-start(f16[4,2,128,128]{3,2,1,0:T(8,128)(2,1)S(1)} %get-tuple-element.5), channel_id=1, source_target_pairs={{0,8},{2,10},{4,12},{6,14},{8,0},{10,2},{12,4},{14,6},{1,9},{3,11}... | collective-permute-start | bytes 786440 | tf_op jit(solution)/shard_map/ppermute | solution.py:18
  6.2 39.4 %collective-permute-start.3 = (f16[4,2,128,128]{3,2,1,0:T(8,128)(2,1)S(1)}, f16[4,2,128,128]{3,2,1,0:T(8,128)(2,1)S(1)}, u32[]{:S(2)}, u32[]{:S(2)}) collective-permute-start(f16[4,2,128,128]{3,2,1,0:T(8,128)(2,1)S(1)} %get-tuple-element.5), channel_id=1, source_target_pairs={{0,2},{2,0},{4,6},{6,4},{8,10},{10,8},{12,14},{14,12},{1,3},{3,1},... | collective-permute-start | bytes 786440 | tf_op jit(solution)/shard_map/ppermute | solution.py:18
  7.7 31.1 %collective-permute-start.5 = (f16[4,2,128,128]{3,2,1,0:T(8,128)(2,1)S(1)}, f16[4,2,128,128]{3,2,1,0:T(8,128)(2,1)S(1)}, u32[]{:S(2)}, u32[]{:S(2)}) collective-permute-start(f16[4,2,128,128]{3,2,1,0:T(8,128)(2,1)S(1)} %get-tuple-element.4), channel_id=1, source_target_pairs={{0,8},{2,10},{4,12},{6,14},{8,0},{10,2},{12,4},{14,6},{1,9},{3,11}... | collective-permute-start | bytes 786440 | tf_op jit(solution)/shard_map/ppermute | solution.py:18
  8.0 37.6 %collective-permute-start.7 = (f16[4,2,128,128]{3,2,1,0:T(8,128)(2,1)S(1)}, f16[4,2,128,128]{3,2,1,0:T(8,128)(2,1)S(1)}, u32[]{:S(2)}, u32[]{:S(2)}) collective-permute-start(f16[4,2,128,128]{3,2,1,0:T(8,128)(2,1)S(1)} %get-tuple-element.4), channel_id=1, source_target_pairs={{0,2},{2,0},{4,6},{6,4},{8,10},{10,8},{12,14},{14,12},{1,3},{3,1},... | collective-permute-start | bytes 786440 | tf_op jit(solution)/shard_map/ppermute | solution.py:18
  8.3 28.4 %collective-permute-start = (s32[4]{0:T(128)S(1)}, s32[4]{0:T(128)S(1)}, u32[]{:S(2)}, u32[]{:S(2)}) collective-permute-start(s32[4]{0:T(128)S(1)} %copy-done.4), channel_id=1, source_target_pairs={{0,4},{2,6},{4,0},{6,2},{8,12},{10,14},{12,8},{14,10},{1,5},{3,7},... | collective-permute-start | bytes 56 | tf_op jit(solution)/shard_map/ppermute | solution.py:18
  10.7 19.7 %all-to-all-start = ((s32[8,1,4]{2,1,0:T(1,128)}), s32[8,1,4]{2,1,0:T(1,128)S(1)}, u32[]{:S(2)}, u32[]{:S(2)}) async-start(s32[8,1,4]{2,1,0:T(1,128)} %broadcast_in_dim.79), calls=%async_computation | async-start | bytes 8192 | tf_op jit(solution)/shard_map/all_to_all | solution.py:22
  15.5 0.7 copy-start.2
  31.8 12.7 %all-to-all-start.1 = ((bf16[8,4,2572]{2,1,0:T(4,128)(2,1)}), bf16[8,4,2572]{2,1,0:T(4,128)(2,1)S(1)}, u32[]{:S(2)}, u32[]{:S(2)}) async-start(bf16[8,4,2572]{2,1,0:T(4,128)(2,1)} %reshape.62), calls=%async_computation.1 | async-start | bytes 344064 | tf_op jit(solution)/shard_map/all_to_all | solution.py:22
  36.7 11.1 %collective-permute-start.2 = (f16[4,2,128,128]{3,2,1,0:T(8,128)(2,1)S(1)}, f16[4,2,128,128]{3,2,1,0:T(8,128)(2,1)S(1)}, u32[]{:S(2)}, u32[]{:S(2)}) collective-permute-start(f16[4,2,128,128]{3,2,1,0:T(8,128)(2,1)S(1)} %collective-permute-done.1), channel_id=1, source_target_pairs={{0,2},{2,0},{4,6},{6,4},{8,10},{10,8},{12,14},{14,12},{1,3},{3,1},... | collective-permute-start | bytes 786440 | tf_op jit(solution)/shard_map/ppermute | solution.py:18
  38.8 13.4 %collective-permute-start.6 = (f16[4,2,128,128]{3,2,1,0:T(8,128)(2,1)S(1)}, f16[4,2,128,128]{3,2,1,0:T(8,128)(2,1)S(1)}, u32[]{:S(2)}, u32[]{:S(2)}) collective-permute-start(f16[4,2,128,128]{3,2,1,0:T(8,128)(2,1)S(1)} %collective-permute-done.5), channel_id=1, source_target_pairs={{0,2},{2,0},{4,6},{6,4},{8,10},{10,8},{12,14},{14,12},{1,3},{3,1},... | collective-permute-start | bytes 786440 | tf_op jit(solution)/shard_map/ppermute | solution.py:18
  44.6 0.7 copy-start.5
  52.2 13.3 %copy-start = (f32[4,4,128,128]{3,2,1,0:T(8,128)S(1)}, f32[4,4,128,128]{3,2,1,0:T(8,128)}, u32[]{:S(2)}) copy-start(f32[4,4,128,128]{3,2,1,0:T(8,128)} %param.7) | copy-start | bytes 3145732
  52.7 9.2 %collective-permute-start.4 = (f16[4,2,128,128]{3,2,1,0:T(8,128)(2,1)S(1)}, f16[4,2,128,128]{3,2,1,0:T(8,128)(2,1)S(1)}, u32[]{:S(2)}, u32[]{:S(2)}) collective-permute-start(f16[4,2,128,128]{3,2,1,0:T(8,128)(2,1)S(1)} %get-tuple-element.7), channel_id=1, source_target_pairs={{0,4},{2,6},{4,0},{6,2},{8,12},{10,14},{12,8},{14,10},{1,5},{3,7},... | collective-permute-start | bytes 786440 | tf_op jit(solution)/shard_map/ppermute | solution.py:18
  54.3 11.2 %collective-permute-start.8 = (f16[4,2,128,128]{3,2,1,0:T(8,128)(2,1)S(1)}, f16[4,2,128,128]{3,2,1,0:T(8,128)(2,1)S(1)}, u32[]{:S(2)}, u32[]{:S(2)}) collective-permute-start(f16[4,2,128,128]{3,2,1,0:T(8,128)(2,1)S(1)} %get-tuple-element.6), channel_id=1, source_target_pairs={{0,4},{2,6},{4,0},{6,2},{8,12},{10,14},{12,8},{14,10},{1,5},{3,7},... | collective-permute-start | bytes 786440 | tf_op jit(solution)/shard_map/ppermute | solution.py:18

commit v3 on v2

--- a/solution.py
+++ b/solution.py
@@ -41,36 +41,58 @@
         head -= ref.shape[1]
 
 
-def column_sum(block):
-    return jnp.sum(block, axis=1, keepdims=True)
+def split(block):
+    high = block.astype(jnp.bfloat16)
+    return high, (block - high.astype(jnp.float32)).astype(jnp.bfloat16)
+
+
+def dot(left, right, axis):
+    return lax.dot_general(
+        left, right, (((axis,), (axis,)), ((), ())), preferred_element_type=jnp.float32
+    )
 
 
 def advance_body(*refs):
     vectors_ref, gain_ref, *parent_refs, readout_ref, states_ref = refs
     rows, heads = states_ref.shape[:2]
-    shape = (HEAD_DIM, HEAD_DIM)
-    diagonal = lax.broadcasted_iota(jnp.int32, shape, 0) == lax.broadcasted_iota(jnp.int32, shape, 1)
+    applied = {}
+    for row in range(rows):
+        for head in range(heads):
+            high, low = split(vectors_ref[row, head])
+            both = jnp.concatenate([high, low], axis=0)
+            parent_high, parent_low = split(next_head(parent_refs, row, head))
+            product = dot(both, parent_high, 1) + dot(both, parent_low, 1)
+            applied[row, head] = product[:8] + product[8:]
+    updates = {}
     for row in range(rows):
         outs = []
         for head in range(heads):
             vecs = vectors_ref[row, head]
-            parent = next_head(parent_refs, row, head)
+            seen = vecs[5:6] * applied[row, head]
             query, key1, key2 = vecs[0:1], vecs[1:2], vecs[2:3]
-            value1, value2 = vecs[3:4], vecs[4:5]
-            beta1, beta2 = vecs[6:7, 0:1], vecs[7:8, 0:1]
-            state = vecs[5:6] * parent
-            part = state * key1
-            step1 = beta1 * column_sum(jnp.where(diagonal, part - value1, part))
-            state = state - step1 * key1
-            part = state * key2
-            step2 = beta2 * column_sum(jnp.where(diagonal, part - value2, part))
-            state = state - step2 * key2
-            states_ref[row, head] = state
-            out = column_sum(state * query)
-            outs.append(jnp.sum(jnp.where(diagonal, out, 0.0), axis=0, keepdims=True))
+            across = jnp.sum(key1 * key2, axis=1, keepdims=True)
+            from1 = jnp.sum(key1 * query, axis=1, keepdims=True)
+            from2 = jnp.sum(key2 * query, axis=1, keepdims=True)
+            step1 = vecs[6:7] * (seen[1:2] - vecs[3:4])
+            step2 = vecs[7:8] * (seen[2:3] - step1 * across - vecs[4:5])
+            outs.append(seen[0:1] - step1 * from1 - step2 * from2)
+            steps = jnp.concatenate([step1, step2], axis=0)
+            updates[row, head] = steps
         out = jnp.concatenate(outs, axis=0)
         scale = lax.rsqrt(jnp.mean(out * out, axis=1, keepdims=True) + 1e-05)
         readout_ref[row] = (gain_ref[...] * out * scale).astype(readout_ref.dtype)
+    blank = jnp.zeros((2, HEAD_DIM), jnp.float32)
+    for row in range(rows):
+        for head in range(heads):
+            vecs = vectors_ref[row, head]
+            steps = updates[row, head]
+            keys = vecs[1:3]
+            steps_high = steps.astype(jnp.bfloat16).astype(jnp.float32)
+            keys_high = keys.astype(jnp.bfloat16).astype(jnp.float32)
+            left = jnp.concatenate([steps_high, steps - steps_high, steps_high, blank], axis=0)
+            right = jnp.concatenate([keys_high, keys_high, keys - keys_high, blank], axis=0)
+            moved = dot(left.astype(jnp.bfloat16), right.astype(jnp.bfloat16), 0)
+            states_ref[row, head] = vecs[5:6] * next_head(parent_refs, row, head) - moved
 
 
 def advance(parents, entries, gate_entries, gain):

time: 75.2 us -> 70.5 us (0.938)
  Pallas kernels: 7.83 us -> 3.13 us
    pallas_call x1, Pallas kernels: 7.83 us -> 3.13 us  [advance(): pl.pallas_call(advance_body, out_shape=(jax.ShapeDtypeStruct((rows, heads...]
where the time goes in v3:
time: 70.5 us; the launch traced here: 70.2 us
  waiting for transfers between devices  36.2 us (51%)
  starting transfers between devices  22 us (31%)
  other arithmetic  4.47 us (6%)
  Pallas kernels  3.13 us (4%)
  local copies, waits for them, and re-layouts  3.08 us (4%)
  between operations  0.81 us (1%)
    all_to_all x2, waiting for transfers between devices, exchange(): lax.all_to_all(block, 'beam', split_axis=0, concat_axis=0, tiled=True)  19.7 us
    ppermute x9, waiting for transfers between devices, swap(): return lax.ppermute(block, 'beam', route)  16.5 us
    ppermute x9, starting transfers between devices, swap(): return lax.ppermute(block, 'beam', route)  12.3 us
    all_to_all x2, starting transfers between devices, exchange(): lax.all_to_all(block, 'beam', split_axis=0, concat_axis=0, tiled=True)  9.66 us
    pallas_call x1, Pallas kernels, advance(): pl.pallas_call(advance_body, out_shape=(jax.ShapeDtypeStruct((rows, heads...  3.13 us
    select_n x1, other arithmetic, step(): parents.append(jnp.where(crossed, block.astype(jnp.float32), mine))  1.52 us
  transfers between devices with their start and end apart: 11, of which 6 were waited for; matrix products, arithmetic and copies ran while one was open for 5% of the time, Pallas kernels for 0%

profile of v3, /device:TPU:0, one launch (start us, length us, event | category | flops | bytes accessed | tf_op | source)
XLA Modules:
  0.0 70.2 jit_solution(5723481992380219037)
XLA Ops:
  0.6 1.4 %slice_convert_fusion = (f16[4,2,128,128]{3,2,1,0:T(8,128)(2,1)S(1)}, f16[4,2,128,128]{3,2,1,0:T(8,128)(2,1)S(1)}) fusion(f32[4,4,128,128]{3,2,1,0:T(8,128)} %param.7), kind=kLoop, calls=%fused_computation.4 | loop fusion | flops 262144 | bytes 1572864 | tf_op jit(solution)/shard_map/convert_element_type | solution.py:160
  2.0 4.1 %collective-permute-start.1 = (f16[4,2,128,128]{3,2,1,0:T(8,128)(2,1)S(1)}, f16[4,2,128,128]{3,2,1,0:T(8,128)(2,1)S(1)}, u32[]{:S(2)}, u32[]{:S(2)}) collective-permute-start(f16[4,2,128,128]{3,2,1,0:T(8,128)(2,1)S(1)} %get-tuple-element.5), channel_id=1, source_target_pairs={{0,8},{2,10},{4,12},{6,14},{8,0},{10,2},{12,4},{14,6},{1,9},{3,11}... | collective-permute-start | bytes 786440 | tf_op jit(solution)/shard_map/ppermute | solution.py:18
  6.2 1.5 %collective-permute-start.3 = (f16[4,2,128,128]{3,2,1,0:T(8,128)(2,1)S(1)}, f16[4,2,128,128]{3,2,1,0:T(8,128)(2,1)S(1)}, u32[]{:S(2)}, u32[]{:S(2)}) collective-permute-start(f16[4,2,128,128]{3,2,1,0:T(8,128)(2,1)S(1)} %get-tuple-element.5), channel_id=1, source_target_pairs={{0,2},{2,0},{4,6},{6,4},{8,10},{10,8},{12,14},{14,12},{1,3},{3,1},... | collective-permute-start | bytes 786440 | tf_op jit(solution)/shard_map/ppermute | solution.py:18
  7.7 0.3 collective-permute-start.5
  8.0 0.3 collective-permute-start.7
  8.3 1.8 %collective-permute-start = (s32[4]{0:T(128)S(1)}, s32[4]{0:T(128)S(1)}, u32[]{:S(2)}, u32[]{:S(2)}) collective-permute-start(s32[4]{0:T(128)S(1)} %copy-done.4), channel_id=1, source_target_pairs={{0,4},{2,6},{4,0},{6,2},{8,12},{10,14},{12,8},{14,10},{1,5},{3,7},... | collective-permute-start | bytes 56 | tf_op jit(solution)/shard_map/ppermute | solution.py:18
  10.1 0.6 broadcast_in_dim.79
  10.7 4.8 %all-to-all-start = ((s32[8,1,4]{2,1,0:T(1,128)}), s32[8,1,4]{2,1,0:T(1,128)S(1)}, u32[]{:S(2)}, u32[]{:S(2)}) async-start(s32[8,1,4]{2,1,0:T(1,128)} %broadcast_in_dim.79), calls=%async_computation | async-start | bytes 8192 | tf_op jit(solution)/shard_map/all_to_all | solution.py:22
  15.6 0.6 copy-done.2
  16.2 14.2 %all-to-all-done = s32[8,1,4]{2,1,0:T(1,128)S(1)} async-done(((s32[8,1,4]{2,1,0:T(1,128)}), s32[8,1,4]{2,1,0:T(1,128)S(1)}, u32[]{:S(2)}, u32[]{:S(2)}) %all-to-all-start) | async-done | bytes 160 | tf_op jit(solution)/shard_map/all_to_all | solution.py:22
  30.5 0.3 convolution_convert_fusion
  30.8 0.2 convolution_convert_fusion.1
  30.9 0.1 copy.15
  31.1 0.7 %reshape.62 = bf16[8,4,2572]{2,1,0:T(4,128)(2,1)} reshape(bf16[32,2572]{1,0:T(8,128)(2,1)S(1)} %pad_maximum_fusion) | data formatting | bytes 329216 | tf_op jit(solution)/shard_map/reshape | solution.py:129
  31.8 4.9 %all-to-all-start.1 = ((bf16[8,4,2572]{2,1,0:T(4,128)(2,1)}), bf16[8,4,2572]{2,1,0:T(4,128)(2,1)S(1)}, u32[]{:S(2)}, u32[]{:S(2)}) async-start(bf16[8,4,2572]{2,1,0:T(4,128)(2,1)} %reshape.62), calls=%async_computation.1 | async-start | bytes 344064 | tf_op jit(solution)/shard_map/all_to_all | solution.py:22
  36.7 2.1 %collective-permute-start.2 = (f16[4,2,128,128]{3,2,1,0:T(8,128)(2,1)S(1)}, f16[4,2,128,128]{3,2,1,0:T(8,128)(2,1)S(1)}, u32[]{:S(2)}, u32[]{:S(2)}) collective-permute-start(f16[4,2,128,128]{3,2,1,0:T(8,128)(2,1)S(1)} %collective-permute-done.1), channel_id=1, source_target_pairs={{0,2},{2,0},{4,6},{6,4},{8,10},{10,8},{12,14},{14,12},{1,3},{3,1},... | collective-permute-start | bytes 786440 | tf_op jit(solution)/shard_map/ppermute | solution.py:18
  38.8 0.1 collective-permute-start.6
  38.9 5.6 %all-to-all-done.1 = bf16[8,4,2572]{2,1,0:T(4,128)(2,1)S(1)} async-done(((bf16[8,4,2572]{2,1,0:T(4,128)(2,1)}), bf16[8,4,2572]{2,1,0:T(4,128)(2,1)S(1)}, u32[]{:S(2)}, u32[]{:S(2)}) %all-to-all-start.1) | async-done | bytes 164640 | tf_op jit(solution)/shard_map/all_to_all | solution.py:22
  44.6 0.1 div.9
  44.7 0.6 copy-done.5
  45.3 0.1 multiply_reduce_fusion
  45.5 0.1 copy.16
  45.6 2.2 %collective-permute-done.2 = f16[4,2,128,128]{3,2,1,0:T(8,128)(2,1)S(1)} collective-permute-done((f16[4,2,128,128]{3,2,1,0:T(8,128)(2,1)S(1)}, f16[4,2,128,128]{3,2,1,0:T(8,128)(2,1)S(1)}, u32[]{:S(2)}, u32[]{:S(2)}) %collective-permute-start.2) | collective-permute-done | bytes 262176 | tf_op jit(solution)/shard_map/ppermute | solution.py:18
  47.8 4.4 %collective-permute-done.6 = f16[4,2,128,128]{3,2,1,0:T(8,128)(2,1)S(1)} collective-permute-done((f16[4,2,128,128]{3,2,1,0:T(8,128)(2,1)S(1)}, f16[4,2,128,128]{3,2,1,0:T(8,128)(2,1)S(1)}, u32[]{:S(2)}, u32[]{:S(2)}) %collective-permute-start.6) | collective-permute-done | bytes 262176 | tf_op jit(solution)/shard_map/ppermute | solution.py:18
  52.2 0.5 select_select_fusion.2
  52.7 1.5 %collective-permute-start.4 = (f16[4,2,128,128]{3,2,1,0:T(8,128)(2,1)S(1)}, f16[4,2,128,128]{3,2,1,0:T(8,128)(2,1)S(1)}, u32[]{:S(2)}, u32[]{:S(2)}) collective-permute-start(f16[4,2,128,128]{3,2,1,0:T(8,128)(2,1)S(1)} %get-tuple-element.7), channel_id=1, source_target_pairs={{0,4},{2,6},{4,0},{6,2},{8,12},{10,14},{12,8},{14,10},{1,5},{3,7},... | collective-permute-start | bytes 786440 | tf_op jit(solution)/shard_map/ppermute | solution.py:18
  54.3 0.6 collective-permute-start.8
  55.0 0.6 pad_maximum_fusion.1.refs_0_
  55.6 6.3 %collective-permute-done.4 = f16[4,2,128,128]{3,2,1,0:T(8,128)(2,1)S(1)} collective-permute-done((f16[4,2,128,128]{3,2,1,0:T(8,128)(2,1)S(1)}, f16[4,2,128,128]{3,2,1,0:T(8,128)(2,1)S(1)}, u32[]{:S(2)}, u32[]{:S(2)}) %collective-permute-start.4) | collective-permute-done | bytes 262176 | tf_op jit(solution)/shard_map/ppermute | solution.py:18
  62.0 3.5 %collective-permute-done.8 = f16[4,2,128,128]{3,2,1,0:T(8,128)(2,1)S(1)} collective-permute-done((f16[4,2,128,128]{3,2,1,0:T(8,128)(2,1)S(1)}, f16[4,2,128,128]{3,2,1,0:T(8,128)(2,1)S(1)}, u32[]{:S(2)}, u32[]{:S(2)}) %collective-permute-start.8) | collective-permute-done | bytes 262176 | tf_op jit(solution)/shard_map/ppermute | solution.py:18
  65.5 1.5 %select_select_fusion = (f32[4,2,128,128]{3,2,1,0:T(8,128)}, f32[4,2,128,128]{3,2,1,0:T(8,128)}) fusion(f16[4,2,128,128]{3,2,1,0:T(8,128)(2,1)S(1)} %collective-permute-done.7, f16[4,2,128,128]{3,2,1,0:T(8,128)(2,1)S(1)} %collective-permute-done.5, f16[4,2,128,128]{3,2,1,0:T(8,128)(2,1)S(1)} %collective-permute-done.6, ...), kind=kLoop, calls=%fused_computation.2 | loop fusion | flops 2097152 | bytes 4194316 | tf_op jit(solution)/shard_map/jit(_where)/select_n | solution.py:172
  67.0 3.1 %advance.1 = (bf16[4,4,128]{2,1,0:T(4,128)(2,1)}, f32[4,4,128,128]{3,2,1,0:T(8,128)}) custom-call(f32[4,4,8,128]{3,2,1,0:T(8,128)} %pad_maximum_fusion.1.refs_0_, f32[4,128]{1,0:T(4,128)} %refs_1_.1, f32[4,2,128,128]{3,2,1,0:T(8,128)} %get-tuple-element.3.refs_2_, f32[4,2,128,128]{3,2,1,0:T(8,128)} %get-tuple-element.2.refs_3_), custom_call_target="tpu_custom_call" | custom-call | tf_op jit(solution)/shard_map/advance/pallas_call | solution.py:101
  (31 shorter events, 0.6 us)
Async XLA Ops:
  0.6 14.9 %copy-start.1 = (bf16[128,4,640]{2,1,0:T(4,128)(2,1)S(1)}, bf16[128,4,640]{2,1,0:T(4,128)(2,1)}, u32[]{:S(2)}) copy-start(bf16[128,4,640]{2,1,0:T(4,128)(2,1)} %param.10) | copy-start | bytes 1966084
  2.0 6.3 %copy-start.4 = (s32[4]{0:T(128)S(1)}, s32[4]{0:T(128)}, u32[]{:S(2)}) copy-start(s32[4]{0:T(128)} %param.8) | copy-start | bytes 52
  2.0 8.1 %copy-start.3 = (s32[4]{0:T(128)S(1)}, s32[4]{0:T(128)}, u32[]{:S(2)}) copy-start(s32[4]{0:T(128)} %param.9) | copy-start | bytes 52
  2.0 34.7 %collective-permute-start.1 = (f16[4,2,128,128]{3,2,1,0:T(8,128)(2,1)S(1)}, f16[4,2,128,128]{3,2,1,0:T(8,128)(2,1)S(1)}, u32[]{:S(2)}, u32[]{:S(2)}) collective-permute-start(f16[4,2,128,128]{3,2,1,0:T(8,128)(2,1)S(1)} %get-tuple-element.5), channel_id=1, source_target_pairs={{0,8},{2,10},{4,12},{6,14},{8,0},{10,2},{12,4},{14,6},{1,9},{3,11}... | collective-permute-start | bytes 786440 | tf_op jit(solution)/shard_map/ppermute | solution.py:18
  6.2 39.4 %collective-permute-start.3 = (f16[4,2,128,128]{3,2,1,0:T(8,128)(2,1)S(1)}, f16[4,2,128,128]{3,2,1,0:T(8,128)(2,1)S(1)}, u32[]{:S(2)}, u32[]{:S(2)}) collective-permute-start(f16[4,2,128,128]{3,2,1,0:T(8,128)(2,1)S(1)} %get-tuple-element.5), channel_id=1, source_target_pairs={{0,2},{2,0},{4,6},{6,4},{8,10},{10,8},{12,14},{14,12},{1,3},{3,1},... | collective-permute-start | bytes 786440 | tf_op jit(solution)/shard_map/ppermute | solution.py:18
  7.7 31.1 %collective-permute-start.5 = (f16[4,2,128,128]{3,2,1,0:T(8,128)(2,1)S(1)}, f16[4,2,128,128]{3,2,1,0:T(8,128)(2,1)S(1)}, u32[]{:S(2)}, u32[]{:S(2)}) collective-permute-start(f16[4,2,128,128]{3,2,1,0:T(8,128)(2,1)S(1)} %get-tuple-element.4), channel_id=1, source_target_pairs={{0,8},{2,10},{4,12},{6,14},{8,0},{10,2},{12,4},{14,6},{1,9},{3,11}... | collective-permute-start | bytes 786440 | tf_op jit(solution)/shard_map/ppermute | solution.py:18
  8.0 37.6 %collective-permute-start.7 = (f16[4,2,128,128]{3,2,1,0:T(8,128)(2,1)S(1)}, f16[4,2,128,128]{3,2,1,0:T(8,128)(2,1)S(1)}, u32[]{:S(2)}, u32[]{:S(2)}) collective-permute-start(f16[4,2,128,128]{3,2,1,0:T(8,128)(2,1)S(1)} %get-tuple-element.4), channel_id=1, source_target_pairs={{0,2},{2,0},{4,6},{6,4},{8,10},{10,8},{12,14},{14,12},{1,3},{3,1},... | collective-permute-start | bytes 786440 | tf_op jit(solution)/shard_map/ppermute | solution.py:18
  8.3 28.4 %collective-permute-start = (s32[4]{0:T(128)S(1)}, s32[4]{0:T(128)S(1)}, u32[]{:S(2)}, u32[]{:S(2)}) collective-permute-start(s32[4]{0:T(128)S(1)} %copy-done.4), channel_id=1, source_target_pairs={{0,4},{2,6},{4,0},{6,2},{8,12},{10,14},{12,8},{14,10},{1,5},{3,7},... | collective-permute-start | bytes 56 | tf_op jit(solution)/shard_map/ppermute | solution.py:18
  10.7 19.7 %all-to-all-start = ((s32[8,1,4]{2,1,0:T(1,128)}), s32[8,1,4]{2,1,0:T(1,128)S(1)}, u32[]{:S(2)}, u32[]{:S(2)}) async-start(s32[8,1,4]{2,1,0:T(1,128)} %broadcast_in_dim.79), calls=%async_computation | async-start | bytes 8192 | tf_op jit(solution)/shard_map/all_to_all | solution.py:22
  15.5 0.7 copy-start.2
  31.8 12.7 %all-to-all-start.1 = ((bf16[8,4,2572]{2,1,0:T(4,128)(2,1)}), bf16[8,4,2572]{2,1,0:T(4,128)(2,1)S(1)}, u32[]{:S(2)}, u32[]{:S(2)}) async-start(bf16[8,4,2572]{2,1,0:T(4,128)(2,1)} %reshape.62), calls=%async_computation.1 | async-start | bytes 344064 | tf_op jit(solution)/shard_map/all_to_all | solution.py:22
  36.7 11.1 %collective-permute-start.2 = (f16[4,2,128,128]{3,2,1,0:T(8,128)(2,1)S(1)}, f16[4,2,128,128]{3,2,1,0:T(8,128)(2,1)S(1)}, u32[]{:S(2)}, u32[]{:S(2)}) collective-permute-start(f16[4,2,128,128]{3,2,1,0:T(8,128)(2,1)S(1)} %collective-permute-done.1), channel_id=1, source_target_pairs={{0,2},{2,0},{4,6},{6,4},{8,10},{10,8},{12,14},{14,12},{1,3},{3,1},... | collective-permute-start | bytes 786440 | tf_op jit(solution)/shard_map/ppermute | solution.py:18
  38.8 13.4 %collective-permute-start.6 = (f16[4,2,128,128]{3,2,1,0:T(8,128)(2,1)S(1)}, f16[4,2,128,128]{3,2,1,0:T(8,128)(2,1)S(1)}, u32[]{:S(2)}, u32[]{:S(2)}) collective-permute-start(f16[4,2,128,128]{3,2,1,0:T(8,128)(2,1)S(1)} %collective-permute-done.5), channel_id=1, source_target_pairs={{0,2},{2,0},{4,6},{6,4},{8,10},{10,8},{12,14},{14,12},{1,3},{3,1},... | collective-permute-start | bytes 786440 | tf_op jit(solution)/shard_map/ppermute | solution.py:18
  44.6 0.7 copy-start.5
  52.2 13.3 %copy-start = (f32[4,4,128,128]{3,2,1,0:T(8,128)S(1)}, f32[4,4,128,128]{3,2,1,0:T(8,128)}, u32[]{:S(2)}) copy-start(f32[4,4,128,128]{3,2,1,0:T(8,128)} %param.7) | copy-start | bytes 3145732
  52.7 9.2 %collective-permute-start.4 = (f16[4,2,128,128]{3,2,1,0:T(8,128)(2,1)S(1)}, f16[4,2,128,128]{3,2,1,0:T(8,128)(2,1)S(1)}, u32[]{:S(2)}, u32[]{:S(2)}) collective-permute-start(f16[4,2,128,128]{3,2,1,0:T(8,128)(2,1)S(1)} %get-tuple-element.7), channel_id=1, source_target_pairs={{0,4},{2,6},{4,0},{6,2},{8,12},{10,14},{12,8},{14,10},{1,5},{3,7},... | collective-permute-start | bytes 786440 | tf_op jit(solution)/shard_map/ppermute | solution.py:18
  54.3 11.2 %collective-permute-start.8 = (f16[4,2,128,128]{3,2,1,0:T(8,128)(2,1)S(1)}, f16[4,2,128,128]{3,2,1,0:T(8,128)(2,1)S(1)}, u32[]{:S(2)}, u32[]{:S(2)}) collective-permute-start(f16[4,2,128,128]{3,2,1,0:T(8,128)(2,1)S(1)} %get-tuple-element.6), channel_id=1, source_target_pairs={{0,4},{2,6},{4,0},{6,2},{8,12},{10,14},{12,8},{14,10},{1,5},{3,7},... | collective-permute-start | bytes 786440 | tf_op jit(solution)/shard_map/ppermute | solution.py:18
